TPU v7x, 256 devices: a whole 4x4x8 slice. The times are simulated.
256 devices in a mesh: ty: 8 (over y, core), tx: 32 (over z, x).
Axes of the slice: x: 4, y: 4, z: 8, core: 2. Of those that a mesh axis runs over, the one named last changes fastest.
Arguments:
- object_field: float32 [2, 2, 3072, 12288], P(None, None, 'ty', 'tx'), may hold values from -5 to 5
- probe_wave: float32 [2, 256, 256], replicated, may hold values from -6 to 6
- prop_phase: float32 [256, 256], replicated, may hold values from -3.140625 to 3.140625
- amplitude: float32 [1024, 256, 256], P(('ty', 'tx')), may hold values from 0.1 to 3
- offsets: int32 [2, 1024], P(None, ('ty', 'tx')), may hold values from 0 to 383, as said below
- live_slots: int32 [1024], P(('ty', 'tx')), may hold values from 0 to 1, as said below
Outputs:
- object_grad: float32 [2, 2, 3072, 12288], P(None, None, 'ty', 'tx')
- probe_grad: float32 [2, 256, 256], replicated
Inputs may be any that keep to these rules, and one draw needn't show every extreme that they name: `offsets`: offsets of row and column of a window inside its device's tile; on devices of the last row of ty the row offset is at most 128, on the last column of tx the column offset likewise, so every window lies inside the object. `live_slots`: each device has between 1 and 4 live slots, in any of its slots; some device has exactly 4.
All inputs are finite; a program needn't handle non-finite values.
Results may differ from a plain program's by a relative error of at most 0.0003.
Values sent between devices are 32-bit elements; how exact they have to be, the bound alone decides.
A program may use at most 128 MiB of HBM per device.

v0:
```python
import math

import jax
import jax.numpy as jnp
from jax import lax
from jax.sharding import PartitionSpec as P


def passed_along(block, axis, distance):
    devices = range(lax.axis_size(axis))
    route = [(i - distance, i) for i in devices if i - distance in devices]
    return lax.ppermute(block, axis, route)


def dft_tables(length):
    indices = jnp.arange(length, dtype=jnp.int32)
    product = indices[:, None] * indices[None, :] % length
    angles = product.astype(jnp.float32) * (2.0 * math.pi / length)
    factor = 1.0 / math.sqrt(length)
    return (jnp.cos(angles) * factor, jnp.sin(angles) * factor)


def matmul(left, right):
    return jnp.dot(left, right, precision=lax.Precision.HIGHEST, preferred_element_type=jnp.float32)


def transform(real_part, imag_part, cosine, sine_table, orient):
    half_real = matmul(real_part, cosine) - orient * matmul(imag_part, sine_table)
    half_imag = matmul(imag_part, cosine) + orient * matmul(real_part, sine_table)
    full_real = matmul(cosine, half_real) - orient * matmul(sine_table, half_imag)
    full_imag = matmul(cosine, half_imag) + orient * matmul(sine_table, half_real)
    return (full_real, full_imag)


def patch_gradient(window, probe_wave, prop_real, prop_imag, measured, cosine, sine_table):
    layers = window.shape[0]
    wave_real, wave_imag = (probe_wave[0], probe_wave[1])
    incident = []
    for layer_index in range(layers):
        trans_real, trans_imag = (window[layer_index, 0], window[layer_index, 1])
        incident.append((wave_real, wave_imag))
        exit_real = trans_real * wave_real - trans_imag * wave_imag
        exit_imag = trans_real * wave_imag + trans_imag * wave_real
        freq_real, freq_imag = transform(exit_real, exit_imag, cosine, sine_table, -1.0)
        if layer_index + 1 < layers:
            kept_real = prop_real * freq_real - prop_imag * freq_imag
            kept_imag = prop_real * freq_imag + prop_imag * freq_real
            wave_real, wave_imag = transform(kept_real, kept_imag, cosine, sine_table, 1.0)
    modulus = jnp.sqrt(freq_real * freq_real + freq_imag * freq_imag + 0.25)
    factor = measured / modulus - 1.0
    back_real, back_imag = transform(
        freq_real * factor, freq_imag * factor, cosine, sine_table, 1.0
    )
    pieces = [None] * layers
    probe_real, probe_imag = (back_real, back_imag)
    for layer_index in reversed(range(layers)):
        inc_real, inc_imag = incident[layer_index]
        trans_real, trans_imag = (window[layer_index, 0], window[layer_index, 1])
        pieces[layer_index] = jnp.stack(
            [
                inc_real * back_real + inc_imag * back_imag,
                inc_real * back_imag - inc_imag * back_real,
            ]
        )
        delta_real = trans_real * back_real + trans_imag * back_imag
        delta_imag = trans_real * back_imag - trans_imag * back_real
        if layer_index > 0:
            upper_real, upper_imag = transform(delta_real, delta_imag, cosine, sine_table, -1.0)
            moved_real = prop_real * upper_real + prop_imag * upper_imag
            moved_imag = prop_real * upper_imag - prop_imag * upper_real
            back_real, back_imag = transform(moved_real, moved_imag, cosine, sine_table, 1.0)
        else:
            probe_real, probe_imag = (delta_real, delta_imag)
    return (jnp.stack(pieces), jnp.stack([probe_real, probe_imag]))


def fetch_sectioned(local, patch):
    right_part = passed_along(local[:, :, :, :patch], "tx", -1)
    widened = jnp.concatenate([local, right_part], axis=3)
    lower_part = passed_along(widened[:, :, :patch, :], "ty", -1)
    return jnp.concatenate([widened, lower_part], axis=2)


def return_sectioned(gathered, tile, patch):
    strip_rows = passed_along(gathered[:, :, tile:, :], "ty", 1)
    rows_kept = gathered[:, :, :tile, :].at[:, :, :patch, :].add(strip_rows)
    right_part = passed_along(rows_kept[:, :, :, tile:], "tx", 1)
    return rows_kept[:, :, :, :tile].at[:, :, :, :patch].add(right_part)


def per_device(object_field, probe_wave, prop_phase, amplitude, offsets, live_slots):
    layers = object_field.shape[0]
    tile = object_field.shape[2]
    patch = probe_wave.shape[1]
    capacity = live_slots.shape[0]
    cosine, sine_table = dft_tables(patch)
    prop_real = jnp.cos(prop_phase)
    prop_imag = jnp.sin(prop_phase)
    extended = fetch_sectioned(object_field, patch)
    visit_order = jnp.arange(capacity, dtype=jnp.int32)
    anchor = jnp.zeros((), jnp.int32)

    def accumulate(position, carry):
        gradient, probe_total = carry
        slot_index = visit_order[position]
        corner = (anchor, anchor, offsets[0, slot_index], offsets[1, slot_index])
        window = lax.dynamic_slice(extended, corner, (layers, 2, patch, patch))
        pieces, probe_piece = patch_gradient(
            window, probe_wave, prop_real, prop_imag, amplitude[slot_index], cosine, sine_table
        )
        weight = live_slots[slot_index].astype(jnp.float32)
        previous = lax.dynamic_slice(gradient, corner, (layers, 2, patch, patch))
        gradient = lax.dynamic_update_slice(gradient, previous + weight * pieces, corner)
        return (gradient, probe_total + weight * probe_piece)

    initial = (jnp.zeros(extended.shape, jnp.float32), jnp.zeros(probe_wave.shape, jnp.float32))
    gradient, probe_total = lax.fori_loop(0, capacity, accumulate, initial)
    owned = return_sectioned(gradient, tile, patch)
    summed = lax.psum(probe_total, ("ty", "tx"))
    scaling = 1.0 / math.sqrt(capacity * lax.axis_size("ty") * lax.axis_size("tx"))
    return (owned, summed * scaling)


def solution(mesh):
    placed = (
        P(None, None, "ty", "tx"),
        P(),
        P(),
        P(("ty", "tx"), None, None),
        P(None, ("ty", "tx")),
        P(("ty", "tx")),
    )
    return jax.shard_map(
        per_device,
        mesh=mesh,
        in_specs=placed,
        out_specs=(P(None, None, "ty", "tx"), P()),
        check_vma=False,
    )
```

profile of v0, /device:TPU:1, one launch (start us, length us, event | category | flops | bytes accessed | tf_op | source)
XLA Modules:
  0.0 829.9 jit_solution(4938146945348766899)
XLA Ops:
  7.2 2.0 copy.15
  10.8 34.4 %collective-permute-done = f32[2,2,384,256]{2,3,1,0:T(8,128)S(1)} collective-permute-done((f32[2,2,384,256]{2,3,1,0:T(8,128)S(1)}, f32[2,2,384,256]{2,3,1,0:T(8,128)S(1)}, u32[]{:S(2)}, u32[]{:S(2)}) %collective-permute-start) | collective-permute-done | bytes 1572896 | tf_op jit(solution)/shard_map/ppermute | solution.py:12
  45.2 1.9 pad_maximum_fusion.1
  47.2 5.5 collective-permute-start.1
  55.5 28.3 %collective-permute-done.1 = f32[2,2,256,640]{2,3,1,0:T(8,128)} collective-permute-done((f32[2,2,256,640]{2,3,1,0:T(8,128)}, f32[2,2,256,640]{2,3,1,0:T(8,128)}, u32[]{:S(2)}, u32[]{:S(2)}) %collective-permute-start.1) | collective-permute-done | bytes 2621472 | tf_op jit(solution)/shard_map/ppermute | solution.py:12
  83.8 5.4 pad_maximum_fusion
  89.1 3.2 broadcast_in_dim.8.clone
  92.3 424.2 %while.21 = (s32[]{:T(128)}, f32[2,2,640,640]{3,2,1,0:T(8,128)}, f32[2,256,256]{1,2,0:T(8,128)}, s32[4]{0:T(128)S(1)}, s32[2,4]{1,0:T(2,128)S(1)}, /*index=5*/s3...) while((s32[]{:T(128)}, f32[2,2,640,640]{3,2,1,0:T(8,128)}, ...), condition=%wide.region_1.2_spmd.clone.clone, body=%wide.region_0.1_spmd.clone.clone.sunk | while | flops 9718464512 | bytes 56623508 | solution.py:117
  112.5 3.0 multiply_subtract_fusion.6
  125.9 2.8 multiply_add_fusion.6
  134.7 1.6 fusion.514
  136.3 1.6 fusion.510
  137.9 1.9 fusion.513
  139.8 2.4 fusion.515
  152.1 3.1 multiply_add_fusion.7
  165.6 2.6 multiply_subtract_fusion.7
  178.6 3.0 add_bitcast_fusion.3
  182.6 1.8 constant_dynamic-slice_fusion.6
  185.2 11.2 %dynamic_update_slice.13 = f32[2,2,640,640]{3,2,1,0:T(8,128)} dynamic-update-slice(f32[2,2,640,640]{3,2,1,0:T(8,128)} %get-tuple-element.784, f32[2,2,256,256]{3,2,1,0:T(8,128)S(1)} %copy.33, s32[]{:T(128)} %constant.139.clone.1..sunk, s32[]{:T(128)} %constant.139.clone.1..sunk, s32[]{:T(128)S(6)} %select_n.330, s32[]{:T(128)S(6)} %select_n.331) | dynamic-update-slice | bytes 2097156 | tf_op jit(solution)/shard_map/while/body/eval_jaxpr/dynamic_update_slice | solution.py:113
  216.8 2.6 multiply_subtract_fusion.6
  229.9 2.9 multiply_add_fusion.6
  240.3 1.6 fusion.510
  241.9 2.1 fusion.513
  244.0 2.4 fusion.515
  256.3 2.8 multiply_add_fusion.7
  269.5 2.7 multiply_subtract_fusion.7
  282.6 3.2 add_bitcast_fusion.3
  285.9 1.9 fusion.534
  287.8 1.8 constant_dynamic-slice_fusion.6
  290.4 12.3 %dynamic_update_slice.13 = f32[2,2,640,640]{3,2,1,0:T(8,128)} dynamic-update-slice(f32[2,2,640,640]{3,2,1,0:T(8,128)} %get-tuple-element.784, f32[2,2,256,256]{3,2,1,0:T(8,128)S(1)} %copy.33, s32[]{:T(128)} %constant.139.clone.1..sunk, s32[]{:T(128)} %constant.139.clone.1..sunk, s32[]{:T(128)S(6)} %select_n.330, s32[]{:T(128)S(6)} %select_n.331) | dynamic-update-slice | bytes 2097156 | tf_op jit(solution)/shard_map/while/body/eval_jaxpr/dynamic_update_slice | solution.py:113
  323.0 2.7 multiply_subtract_fusion.6
  336.0 3.0 multiply_add_fusion.6
  345.0 1.6 fusion.514
  346.7 1.6 fusion.510
  348.3 1.8 fusion.513
  350.2 2.4 fusion.515
  362.5 2.9 multiply_add_fusion.7
  375.7 2.9 multiply_subtract_fusion.7
  388.9 3.0 add_bitcast_fusion.3
  392.0 1.9 fusion.534
  393.9 1.8 constant_dynamic-slice_fusion.6
  396.5 11.6 %dynamic_update_slice.13 = f32[2,2,640,640]{3,2,1,0:T(8,128)} dynamic-update-slice(f32[2,2,640,640]{3,2,1,0:T(8,128)} %get-tuple-element.784, f32[2,2,256,256]{3,2,1,0:T(8,128)S(1)} %copy.33, s32[]{:T(128)} %constant.139.clone.1..sunk, s32[]{:T(128)} %constant.139.clone.1..sunk, s32[]{:T(128)S(6)} %select_n.330, s32[]{:T(128)S(6)} %select_n.331) | dynamic-update-slice | bytes 2097156 | tf_op jit(solution)/shard_map/while/body/eval_jaxpr/dynamic_update_slice | solution.py:113
  428.5 2.9 multiply_subtract_fusion.6
  441.8 2.8 multiply_add_fusion.6
  452.2 1.6 fusion.510
  453.8 1.9 fusion.513
  455.7 2.4 fusion.515
  468.0 3.1 multiply_add_fusion.7
  481.4 2.6 multiply_subtract_fusion.7
  494.4 3.0 add_bitcast_fusion.3
  497.5 1.9 fusion.534
  499.4 1.8 constant_dynamic-slice_fusion.6
  502.1 12.0 %dynamic_update_slice.13 = f32[2,2,640,640]{3,2,1,0:T(8,128)} dynamic-update-slice(f32[2,2,640,640]{3,2,1,0:T(8,128)} %get-tuple-element.784, f32[2,2,256,256]{3,2,1,0:T(8,128)S(1)} %copy.33, s32[]{:T(128)} %constant.139.clone.1..sunk, s32[]{:T(128)} %constant.139.clone.1..sunk, s32[]{:T(128)S(6)} %select_n.330, s32[]{:T(128)S(6)} %select_n.331) | dynamic-update-slice | bytes 2097156 | tf_op jit(solution)/shard_map/while/body/eval_jaxpr/dynamic_update_slice | solution.py:113
  516.6 1.9 slice.146
  518.5 3.2 collective-permute-start.2
  521.8 2.4 slice.144
  524.1 26.2 %collective-permute-done.2 = f32[2,2,256,640]{3,2,1,0:T(8,128)S(1)} collective-permute-done((f32[2,2,256,640]{3,2,1,0:T(8,128)S(1)}, f32[2,2,256,640]{3,2,1,0:T(8,128)S(1)}, u32[]{:S(2)}, u32[]{:S(2)}) %collective-permute-start.2) | collective-permute-done | bytes 2621472 | tf_op jit(solution)/shard_map/ppermute | solution.py:12
  550.3 2.1 add_dynamic-update-slice_fusion
  552.4 1.9 copy-done
  554.4 2.4 collective-permute-start.3
  556.9 2.0 copy.22
  558.9 257.1 %all-reduce.2.cloned.1.call-done = f32[2,256,256]{2,1,0:T(8,128)} async-done(((f32[2,256,256]{2,1,0:T(8,128)}), f32[2,256,256]{2,1,0:T(8,128)}) %all-reduce.2.cloned.1.call-update) | async-done | bytes 524304 | tf_op jit(solution)/shard_map/psum | solution.py:119
  816.0 1.9 broadcast_multiply_fusion
  817.9 1.8 slice.163
  (216 shorter events, 256.4 us)
Async XLA Ops:
  7.2 808.9 %all-reduce.2.cloned.1.call-start = ((), (), s32[]{:S(2)}) async-start(), calls=%async_computation | async-start | bytes 1048576 | tf_op jit(solution)/shard_map/psum | solution.py:119
  9.4 43.4 %copy-start.4 = (f32[256,256]{1,0:T(8,128)S(1)}, f32[256,256]{1,0:T(8,128)}, u32[]{:S(2)}) copy-start(f32[256,256]{1,0:T(8,128)} %param.14) | copy-start | bytes 786436
  9.4 43.5 %copy-start.3 = (f32[2,256,256]{2,1,0:T(8,128)S(1)}, f32[2,256,256]{2,1,0:T(8,128)}, u32[]{:S(2)}) copy-start(f32[2,256,256]{2,1,0:T(8,128)} %param.13) | copy-start | bytes 1572868
  9.4 35.8 %collective-permute-start = (f32[2,2,384,256]{2,3,1,0:T(8,128)S(1)}, f32[2,2,384,256]{2,3,1,0:T(8,128)S(1)}, u32[]{:S(2)}, u32[]{:S(2)}) collective-permute-start(f32[2,2,384,256]{2,3,1,0:T(8,128)S(1)} %slice.162), channel_id=1, source_target_pairs={{1,0},{2,1},{3,2},{4,3},{5,4},{6,5},{7,6},{8,7},{9,8},{10,9},{11,1... | collective-permute-start | bytes 4718600 | tf_op jit(solution)/shard_map/ppermute | solution.py:12
  45.2 2.0 copy-start.1
  47.2 36.5 %collective-permute-start.1 = (f32[2,2,256,640]{2,3,1,0:T(8,128)}, f32[2,2,256,640]{2,3,1,0:T(8,128)}, u32[]{:S(2)}, u32[]{:S(2)}) collective-permute-start(f32[2,2,256,640]{2,3,1,0:T(8,128)} %pad_maximum_fusion.1), channel_id=1, source_target_pairs={{32,0},{64,32},{96,64},{128,96},{160,128},{192,160},{224,192},{33,... | collective-permute-start | bytes 7864328 | tf_op jit(solution)/shard_map/ppermute | solution.py:12
  89.1 3.2 copy-start.5
  89.1 3.2 copy-start.6
  518.5 31.8 %collective-permute-start.2 = (f32[2,2,256,640]{3,2,1,0:T(8,128)S(1)}, f32[2,2,256,640]{3,2,1,0:T(8,128)S(1)}, u32[]{:S(2)}, u32[]{:S(2)}) collective-permute-start(f32[2,2,256,640]{3,2,1,0:T(8,128)S(1)} %slice.146), channel_id=1, source_target_pairs={{0,32},{32,64},{64,96},{96,128},{128,160},{160,192},{192,224},{1,3... | collective-permute-start | bytes 7864328 | tf_op jit(solution)/shard_map/ppermute | solution.py:12
  552.4 1.9 copy-start
  554.4 265.3 %collective-permute-start.3 = (f32[2,2,384,256]{3,2,1,0:T(8,128)S(1)}, f32[2,2,384,256]{3,2,1,0:T(8,128)S(1)}, u32[]{:S(2)}, u32[]{:S(2)}) collective-permute-start(f32[2,2,384,256]{3,2,1,0:T(8,128)S(1)} %slice.165), channel_id=1, source_target_pairs={{0,1},{1,2},{2,3},{3,4},{4,5},{5,6},{6,7},{7,8},{8,9},{9,10},{10,1... | collective-permute-start | bytes 4718600 | tf_op jit(solution)/shard_map/ppermute | solution.py:12
  821.4 1.4 copy-start.2
Sparse Core Ops, SparseCore 0:
  559.0 256.9 all-reduce.1
where the time goes:
time: 836 us; the launch traced here: 830 us
  waiting for transfers between devices  346 us (41%)
  matrix products  316 us (38%)
  local copies, waits for them, and re-layouts  84 us (10%)
  loops' own time  30.6 us (4%)
  other arithmetic  26.3 us (3%)
  between operations  14.5 us (2%)
  starting transfers between devices  12.6 us (2%)
    dot_general x192, matrix products, matmul(): jnp.dot(left, right, precision=lax.Precision.HIGHEST, preferred_element_t...  316 us
    psum x1, waiting for transfers between devices, per_device(): summed = lax.psum(probe_total, ('ty', 'tx'))  257 us
    ppermute x4, waiting for transfers between devices, passed_along(): return lax.ppermute(block, axis, route)  88.9 us
    dynamic_update_slice x8, local copies, waits for them, and re-layouts, accumulate(): lax.dynamic_update_slice(gradient, previous + weight * pieces, corner)  48.4 us
    another operation x1, loops' own time, per_device(): gradient, probe_total = lax.fori_loop(0, capacity, accumulate, initial)  30.6 us
  transfers between devices with their start and end apart: 5, of which 4 were waited for; matrix products, arithmetic and copies ran while one was open for 1% of the time, Pallas kernels for 0%

commit v1 on v0

v1 whole, which is shorter than its diff:
```python
import functools
import math

import jax
import jax.numpy as jnp
import ml_dtypes
import numpy as np
from jax import lax
from jax.experimental import pallas as pl
from jax.experimental.pallas import tpu as pltpu
from jax.sharding import PartitionSpec as P

F32 = jnp.float32
BF16 = jnp.bfloat16
MESH = pl.DeviceIdType.MESH
LANES = 128
INNER = 4


def halves(table):
    high = table.astype(np.float32).astype(ml_dtypes.bfloat16)
    low = (table - high.astype(np.float64)).astype(ml_dtypes.bfloat16)
    return np.stack([high, low])


def dft_halves(length):
    half = length // 2
    sample = np.arange(half)[:, None]
    tables = []
    for parity in range(2):
        freq = 2 * np.arange(half)[None, :] + parity
        angle = 2.0 * math.pi * ((sample * freq) % length) / length
        cosine = np.cos(angle) / math.sqrt(length)
        sine = np.sin(angle) / math.sqrt(length)
        full = np.block([[cosine, -sine], [sine, cosine]])
        tables.append(np.stack([halves(full), halves(full.T)]))
    return np.stack(tables)


def even_odd(length):
    order = np.concatenate([np.arange(0, length, 2), np.arange(1, length, 2)])
    chosen = np.zeros((length, length), np.float32)
    chosen[order, np.arange(length)] = 1.0
    return np.stack([chosen, chosen.T]).astype(ml_dtypes.bfloat16)


def split(value):
    high = value.astype(BF16)
    low = (value - high.astype(F32)).astype(BF16)
    return high, low


def product(left, right):
    return jnp.dot(left, right, preferred_element_type=F32)


def from_right(value, table):
    high, low = split(value)
    left = jnp.concatenate([high, low, high], axis=1)
    return product(left, jnp.concatenate([table[0], table[0], table[1]], axis=0))


def from_left(table, value):
    high, low = split(value)
    right = jnp.concatenate([high, low, high], axis=0)
    return product(jnp.concatenate([table[0], table[0], table[1]], axis=1), right)


def thirds(value):
    high = value.astype(BF16)
    rest = value - high.astype(F32)
    middle = rest.astype(BF16)
    low = (rest - middle.astype(F32)).astype(BF16)
    return high, middle, low


def reorder(value, chosen, chosen_t):
    pieces = thirds(value)
    across = sum(product(piece, chosen) for piece in pieces)
    return sum(product(chosen_t, piece) for piece in thirds(across))


def beside(left, right):
    return jnp.concatenate([left, right], axis=1)


def above(top, bottom):
    return jnp.concatenate([top, bottom], axis=0)


def forward(real, imag, tables):
    n = LANES
    even = from_right(
        beside(real[:, :n] + real[:, n:], imag[:, :n] + imag[:, n:]), tables[0, 0]
    )
    odd = from_right(
        beside(real[:, :n] - real[:, n:], imag[:, :n] - imag[:, n:]), tables[1, 0]
    )
    real = beside(even[:, :n], odd[:, :n])
    imag = beside(even[:, n:], odd[:, n:])
    even = from_left(tables[0, 1], above(real[:n] + real[n:], imag[:n] + imag[n:]))
    odd = from_left(tables[1, 1], above(real[:n] - real[n:], imag[:n] - imag[n:]))
    return above(even[:n], odd[:n]), above(even[n:], odd[n:])


def backward(real, imag, tables):
    n = LANES
    even = from_left(tables[0, 0], above(real[:n], imag[:n]))
    odd = from_left(tables[1, 0], above(real[n:], imag[n:]))
    total, change = even + odd, even - odd
    real, imag = above(total[:n], change[:n]), above(total[n:], change[n:])
    even = from_right(beside(real[:, :n], imag[:, :n]), tables[0, 1])
    odd = from_right(beside(real[:, n:], imag[:, n:]), tables[1, 1])
    total, change = even + odd, even - odd
    return beside(total[:, :n], change[:, :n]), beside(total[:, n:], change[:, n:])


def step_kernel(
    n_ty,
    n_tx,
    obj,
    probe,
    phase,
    amplitude,
    offsets,
    live,
    tables,
    chosen,
    grad,
    probe_grad,
    wide_first,
    wide_second,
    padded,
    total,
    from_left_tile,
    from_above,
    psi,
    trans,
    prop,
    target,
    local_sem,
    get_send,
    get_recv,
    put_send,
    put_recv,
    out_sem,
):
    wide = (wide_first, wide_second)
    layers, _, tile, _ = obj.shape
    patch = probe.shape[1]
    slots = amplitude.shape[0]
    lane_tiles = tile // LANES
    strip_tiles = patch // LANES
    all_tiles = lane_tiles + strip_tiles
    lower = tile - patch
    ty, tx = lax.axis_index("ty"), lax.axis_index("tx")
    left = (ty, lax.rem(tx + n_tx - 1, n_tx))
    right = (ty, lax.rem(tx + 1, n_tx))
    up = (lax.rem(ty + n_ty - 1, n_ty), tx)
    down = (lax.rem(ty + 1, n_ty), tx)

    barrier = pltpu.get_barrier_semaphore()
    for neighbour in (left, right, up, down):
        pl.semaphore_signal(barrier, inc=1, device_id=neighbour, device_id_type=MESH)
    pl.semaphore_wait(barrier, 4)

    def remote(source, destination, send, recv, device):
        return pltpu.make_async_remote_copy(
            src_ref=source,
            dst_ref=destination,
            send_sem=send,
            recv_sem=recv,
            device_id=device,
            device_id_type=MESH,
        )

    def columns(j):
        return pl.ds(j * LANES, LANES)

    def get(s, source, destination, index, device):
        return remote(source, destination, get_send.at[s, index], get_recv.at[s, index], device)

    def get_right(s, block):
        first, size = ((0, patch), (patch, lower))[block]
        return [
            get(
                s,
                obj.at[s, :, pl.ds(first, size), columns(j)],
                wide[s].at[:, lane_tiles + j, pl.ds(first, size), :],
                block * strip_tiles + j,
                left,
            )
            for j in range(strip_tiles)
        ]

    def get_below(s):
        return [
            get(
                s,
                obj.at[s, :, pl.ds(0, patch), columns(j)],
                wide[s].at[:, j, pl.ds(tile, patch), :],
                2 * strip_tiles + j,
                up,
            )
            for j in range(lane_tiles)
        ]

    def get_corner(s):
        corner = pl.ds(lane_tiles, strip_tiles)
        return get(
            s,
            wide[s].at[:, corner, pl.ds(0, patch), :],
            wide[s].at[:, corner, pl.ds(tile, patch), :],
            2 * strip_tiles + lane_tiles,
            up,
        )

    def start_get(s):
        for copy in get_right(s, 0) + get_below(s) + get_right(s, 1):
            copy.start()

    def relay_get(s):
        for copy in get_right(s, 0):
            copy.wait_recv()
        get_corner(s).start()

    def finish_get(s):
        for copy in get_right(s, 1) + get_below(s) + [get_corner(s)]:
            copy.wait_recv()

    def sent_get(s):
        for copy in get_right(s, 0) + get_right(s, 1) + get_below(s) + [get_corner(s)]:
            copy.wait_send()

    def put(s, source, destination, index, device):
        return remote(source, destination, put_send.at[s, index], put_recv.at[s, index], device)

    def put_rows(s, first, size, index):
        return put(
            s,
            total.at[s, :, pl.ds(lane_tiles, strip_tiles), pl.ds(first, size), :],
            from_left_tile.at[s, :, :, pl.ds(first, size), :],
            index,
            right,
        )

    def put_below(s, first, count, index):
        return put(
            s,
            total.at[s, :, pl.ds(first, count), pl.ds(tile, patch), :],
            from_above.at[s, :, pl.ds(first, count), :, :],
            index,
            down,
        )

    def put_part(s, index):
        if index == 0:
            return put_below(s, lane_tiles, strip_tiles, index)
        if index == 1:
            return put_rows(s, patch, lower, index)
        if index == 2:
            return put_below(s, 0, lane_tiles, index)
        return put_rows(s, 0, patch, index)

    def start_put(s):
        for index in range(3):
            put_part(s, index).start()

    def relay_put(s):
        put_part(s, 0).wait_recv()

        def add_rows(block, carry):
            rows = pl.ds(pl.multiple_of(block * 64, 64), 64)
            for part in range(2):
                for j in range(lane_tiles, all_tiles):
                    total[s, part, j, rows, :] += from_above[s, part, j, rows, :]
            return carry

        lax.fori_loop(0, patch // 64, add_rows, 0)
        put_part(s, 3).start()

    def out_copies(s):
        return [
            pltpu.make_async_copy(
                total.at[s, :, j, pl.ds(0, tile), :],
                grad.at[s, :, :, columns(j)],
                out_sem.at[s, j],
            )
            for j in range(lane_tiles)
        ]

    def finish_put(s):
        for index in range(1, 4):
            put_part(s, index).wait_recv()

        def add_rows(block, carry):
            rows = pl.ds(pl.multiple_of(block * 64, 64), 64)
            for part in range(2):
                for j in range(strip_tiles):
                    total[s, part, j, rows, :] += from_left_tile[s, part, j, rows, :]
            return carry

        def add_above(block, carry):
            rows = pl.ds(pl.multiple_of(block * 64, 64), 64)
            for part in range(2):
                for j in range(lane_tiles):
                    total[s, part, j, rows, :] += from_above[s, part, j, rows, :]
            return carry

        lax.fori_loop(0, tile // 64, add_rows, 0)
        lax.fori_loop(0, patch // 64, add_above, 0)
        for copy in out_copies(s):
            copy.start()

    start_get(0)
    local = [
        pltpu.make_async_copy(
            obj.at[s, :, :, columns(j)], wide[s].at[:, j, pl.ds(0, tile), :], local_sem.at[s, j]
        )
        for s in range(layers)
        for j in range(lane_tiles)
    ]
    for copy in local:
        copy.start()

    def clear(q, carry):
        for part in range(2):
            for j in range(strip_tiles + 1):
                padded[q, part, j, pl.ds(0, tile), :] = jnp.zeros((tile, LANES), F32)
                padded[q, part, j, pl.ds(tile + patch, tile), :] = jnp.zeros((tile, LANES), F32)
        return carry

    lax.fori_loop(0, slots, clear, 0)

    def order_target(q, carry):
        target[q] = reorder(amplitude[q], chosen[0], chosen[1])
        return carry

    lax.fori_loop(0, slots, order_target, 0)
    angle = reorder(phase[...], chosen[0], chosen[1])
    prop[0] = jnp.cos(angle)
    prop[1] = jnp.sin(angle)
    for copy in local:
        copy.wait()
    relay_get(0)
    finish_get(0)
    sent_get(0)
    start_get(1)

    lane = lax.broadcasted_iota(jnp.int32, (patch, LANES), 1)

    def place(q):
        row, column = offsets[0, q], offsets[1, q]
        return row, lax.shift_right_logical(column, 7), lax.bitwise_and(column, LANES - 1)

    def window(s, part, q):
        row, tile_index, shift = place(q)
        back = lax.bitwise_and(LANES - shift, LANES - 1)
        rolled = [
            pltpu.roll(wide[s][part, tile_index + k, pl.ds(row, patch), :], back, 1)
            for k in range(strip_tiles + 1)
        ]
        keep = lane < LANES - shift
        return jnp.concatenate(
            [jnp.where(keep, rolled[k], rolled[k + 1]) for k in range(strip_tiles)], axis=1
        )

    def deposit(q, part, piece):
        _, _, shift = place(q)
        rolled = [
            pltpu.roll(piece[:, k * LANES : (k + 1) * LANES], shift, 1) for k in range(strip_tiles)
        ]
        rolled = [jnp.zeros((patch, LANES), F32)] + rolled + [jnp.zeros((patch, LANES), F32)]
        keep = lane >= shift
        for k in range(strip_tiles + 1):
            padded[q, part, k, pl.ds(tile, patch), :] = jnp.where(keep, rolled[k + 1], rolled[k])

    def gather(s, tiles, first, size):
        places = [place(q) for q in range(slots)]
        alive = [live[q].astype(F32) for q in range(slots)]

        def rows_of(block, carry):
            begin = first + block * 64
            for j in tiles:
                weights, sources = [], []
                for q in range(slots):
                    inside = j - places[q][1]
                    valid = jnp.logical_and(inside >= 0, inside <= strip_tiles)
                    weights.append(jnp.where(valid, alive[q], 0.0))
                    sources.append(jnp.clip(inside, 0, strip_tiles))
                for part in range(2):
                    value = jnp.zeros((64, LANES), F32)
                    for q in range(slots):
                        rows = pl.ds(tile - places[q][0] + begin, 64)
                        value += weights[q] * padded[q, part, sources[q], rows, :]
                    total[s, part, j, pl.ds(pl.multiple_of(begin, 64), 64), :] = value
            return carry

        lax.fori_loop(0, size // 64, rows_of, 0)

    def first_layer(q, carry):
        trans_real, trans_imag = window(0, 0, q), window(0, 1, q)
        trans[q, 0], trans[q, 1] = trans_real, trans_imag
        freq_real, freq_imag = forward(
            trans_real * probe[0] - trans_imag * probe[1],
            trans_real * probe[1] + trans_imag * probe[0],
            tables,
        )
        psi[q, 0], psi[q, 1] = backward(
            prop[0] * freq_real - prop[1] * freq_imag,
            prop[0] * freq_imag + prop[1] * freq_real,
            tables,
        )
        return carry

    lax.fori_loop(0, slots, first_layer, 0)
    relay_get(1)
    finish_get(1)
    sent_get(1)

    def second_layer(q, carry):
        trans_real, trans_imag = window(1, 0, q), window(1, 1, q)
        wave_real, wave_imag = psi[q, 0], psi[q, 1]
        freq_real, freq_imag = forward(
            trans_real * wave_real - trans_imag * wave_imag,
            trans_real * wave_imag + trans_imag * wave_real,
            tables,
        )
        energy = freq_real * freq_real + freq_imag * freq_imag + 0.25
        factor = target[q] / jnp.sqrt(energy) - 1.0
        back_real, back_imag = backward(freq_real * factor, freq_imag * factor, tables)
        wave_real, wave_imag = psi[q, 0], psi[q, 1]
        deposit(q, 0, wave_real * back_real + wave_imag * back_imag)
        deposit(q, 1, wave_real * back_imag - wave_imag * back_real)
        trans_real, trans_imag = window(1, 0, q), window(1, 1, q)
        psi[q, 0] = trans_real * back_real + trans_imag * back_imag
        psi[q, 1] = trans_real * back_imag - trans_imag * back_real
        return carry

    lax.fori_loop(0, slots, second_layer, 0)
    strip = range(lane_tiles, all_tiles)
    inner = range(lane_tiles)

    def send_edges(s):
        gather(s, strip, 0, tile + patch)
        gather(s, inner, tile, patch)
        start_put(s)
        gather(s, inner, 0, tile)

    send_edges(1)
    probe_grad[...] = jnp.zeros(probe_grad.shape, F32)

    def third_layer(q, carry):
        freq_real, freq_imag = forward(psi[q, 0], psi[q, 1], tables)
        back_real, back_imag = backward(
            prop[0] * freq_real + prop[1] * freq_imag,
            prop[0] * freq_imag - prop[1] * freq_real,
            tables,
        )
        deposit(q, 0, probe[0] * back_real + probe[1] * back_imag)
        deposit(q, 1, probe[0] * back_imag - probe[1] * back_real)
        weight = live[q].astype(F32)
        probe_grad[0] += weight * (trans[q, 0] * back_real + trans[q, 1] * back_imag)
        probe_grad[1] += weight * (trans[q, 0] * back_imag - trans[q, 1] * back_real)
        return carry

    lax.fori_loop(0, slots // 2, third_layer, 0)
    relay_put(1)
    lax.fori_loop(slots // 2, slots, third_layer, 0)
    send_edges(0)
    finish_put(1)
    relay_put(0)
    finish_put(0)
    for s in range(layers):
        for index in range(4):
            put_part(s, index).wait_send()
        for copy in out_copies(s):
            copy.wait()


def step_call(n_ty, n_tx, *operands):
    obj, probe, _, amplitude, _, _, _, _ = operands
    layers, _, tile, _ = obj.shape
    patch = probe.shape[1]
    slots = amplitude.shape[0]
    lane_tiles, strip_tiles = tile // LANES, patch // LANES
    all_tiles = lane_tiles + strip_tiles
    gets = 2 * strip_tiles + lane_tiles + 1
    vmem = pl.BlockSpec(memory_space=pltpu.VMEM)
    smem = pl.BlockSpec(memory_space=pltpu.SMEM)
    whole = pl.BlockSpec(memory_space=pl.ANY)
    return pl.pallas_call(
        functools.partial(step_kernel, n_ty, n_tx),
        name="step",
        out_shape=(
            jax.ShapeDtypeStruct(obj.shape, F32),
            jax.ShapeDtypeStruct(probe.shape, F32),
        ),
        in_specs=[whole, vmem, vmem, vmem, smem, smem, vmem, vmem],
        out_specs=(whole, vmem),
        scratch_shapes=[
            pltpu.VMEM((2, all_tiles, tile + patch, LANES), F32),
            pltpu.VMEM((2, all_tiles, tile + patch, LANES), F32),
            pltpu.VMEM((slots, 2, strip_tiles + 1, 2 * tile + patch, LANES), F32),
            pltpu.VMEM((layers, 2, all_tiles, tile + patch, LANES), F32),
            pltpu.VMEM((layers, 2, strip_tiles, tile, LANES), F32),
            pltpu.VMEM((layers, 2, all_tiles, patch, LANES), F32),
            pltpu.VMEM((slots, 2, patch, patch), F32),
            pltpu.VMEM((slots, 2, patch, patch), F32),
            pltpu.VMEM((2, patch, patch), F32),
            pltpu.VMEM((slots, patch, patch), F32),
            pltpu.SemaphoreType.DMA((layers, lane_tiles)),
            pltpu.SemaphoreType.DMA((layers, gets)),
            pltpu.SemaphoreType.DMA((layers, gets)),
            pltpu.SemaphoreType.DMA((layers, 4)),
            pltpu.SemaphoreType.DMA((layers, 4)),
            pltpu.SemaphoreType.DMA((layers, lane_tiles)),
        ],
        compiler_params=pltpu.CompilerParams(
            collective_id=0, has_side_effects=True, vmem_limit_bytes=60 * 1024 * 1024
        ),
    )(*operands)


def sum_kernel(
    n_ty, n_tx, scaling, part, whole, near, far, near_send, near_recv, far_send, far_recv,
    last_send, last_recv,
):
    near_count, far_count = n_ty * INNER, n_tx // INNER
    ty, tx = lax.axis_index("ty"), lax.axis_index("tx")
    inner, outer = lax.rem(tx, INNER), lax.div(tx, INNER)
    mine = ty * INNER + inner

    def near_peer(step):
        index = lax.rem(mine + step, near_count)
        return index, (lax.div(index, INNER), outer * INNER + lax.rem(index, INNER))

    def far_peer(step):
        index = lax.rem(outer + step, far_count)
        return index, (ty, index * INNER + inner)

    barrier = pltpu.get_barrier_semaphore()

    def greet_near(step, carry):
        pl.semaphore_signal(barrier, inc=1, device_id=near_peer(step)[1], device_id_type=MESH)
        return carry

    def greet_far(step, carry):
        pl.semaphore_signal(barrier, inc=1, device_id=far_peer(step)[1], device_id_type=MESH)
        return carry

    lax.fori_loop(1, near_count, greet_near, 0)
    lax.fori_loop(1, far_count, greet_far, 0)
    pl.semaphore_wait(barrier, near_count + far_count - 2)

    def remote(source, destination, send, recv, device):
        return pltpu.make_async_remote_copy(
            src_ref=source,
            dst_ref=destination,
            send_sem=send,
            recv_sem=recv,
            device_id=device,
            device_id_type=MESH,
        )

    def exchange(count, peer, make):
        def start(step, carry):
            make(*peer(step))[0].start()
            return carry

        def wait(step, carry):
            make(*peer(step))[1].wait_recv()
            return carry

        def sent(step, carry):
            make(*peer(step))[0].wait_send()
            return carry

        lax.fori_loop(1, count, start, 0)
        lax.fori_loop(1, count, wait, 0)
        return lambda: lax.fori_loop(1, count, sent, 0)

    def scatter(index, device):
        return (
            remote(part.at[index], near.at[mine], near_send.at[index], near_recv.at[mine], device),
            remote(part.at[mine], near.at[index], near_send.at[index], near_recv.at[index], device),
        )

    near[mine] = part[mine]
    done_near = exchange(near_count, near_peer, scatter)
    value = near[0]
    for index in range(1, near_count):
        value += near[index]
    far[outer] = value

    def across(index, device):
        return (
            remote(far.at[outer], far.at[outer], far_send.at[index], far_recv.at[outer], device),
            remote(far.at[outer], far.at[index], far_send.at[index], far_recv.at[index], device),
        )

    done_far = exchange(far_count, far_peer, across)
    value = far[0]
    for index in range(1, far_count):
        value += far[index]
    whole[mine] = value * scaling

    def spread(index, device):
        return (
            remote(
                whole.at[mine], whole.at[mine], last_send.at[index], last_recv.at[mine], device
            ),
            remote(
                whole.at[mine], whole.at[index], last_send.at[index], last_recv.at[index], device
            ),
        )

    done_last = exchange(near_count, near_peer, spread)
    done_near()
    done_far()
    done_last()


def sum_call(n_ty, n_tx, scaling, value):
    near_count, far_count = n_ty * INNER, n_tx // INNER
    width = value.shape[-1]
    rows = value.size // width // near_count
    vmem = pl.BlockSpec(memory_space=pltpu.VMEM)
    sems = pltpu.SemaphoreType.DMA
    summed = pl.pallas_call(
        functools.partial(sum_kernel, n_ty, n_tx, scaling),
        name="sum_probe",
        out_shape=jax.ShapeDtypeStruct((near_count, rows, width), F32),
        in_specs=[vmem],
        out_specs=vmem,
        scratch_shapes=[
            pltpu.VMEM((near_count, rows, width), F32),
            pltpu.VMEM((far_count, rows, width), F32),
            sems((near_count,)),
            sems((near_count,)),
            sems((far_count,)),
            sems((far_count,)),
            sems((near_count,)),
            sems((near_count,)),
        ],
        compiler_params=pltpu.CompilerParams(collective_id=1, has_side_effects=True),
    )(value.reshape(near_count, rows, width))
    return summed.reshape(value.shape)


def solution(mesh):
    n_ty, n_tx = mesh.shape["ty"], mesh.shape["tx"]

    def per_device(object_field, probe_wave, prop_phase, amplitude, offsets, live_slots):
        patch = probe_wave.shape[1]
        owned, probe_part = step_call(
            n_ty,
            n_tx,
            object_field,
            probe_wave,
            prop_phase,
            amplitude,
            offsets,
            live_slots,
            jnp.asarray(dft_halves(patch)),
            jnp.asarray(even_odd(patch)),
        )
        scaling = 1.0 / math.sqrt(live_slots.shape[0] * n_ty * n_tx)
        return owned, sum_call(n_ty, n_tx, scaling, probe_part)

    placed = (
        P(None, None, "ty", "tx"),
        P(),
        P(),
        P(("ty", "tx"), None, None),
        P(None, ("ty", "tx")),
        P(("ty", "tx")),
    )
    return jax.shard_map(
        per_device,
        mesh=mesh,
        in_specs=placed,
        out_specs=(P(None, None, "ty", "tx"), P()),
        check_vma=False,
    )
```

time: 836 us -> 137 us (0.16)
  waiting for transfers between devices: 346 us -> 0 us
  matrix products: 316 us -> 0 us
  Pallas kernels: 0 us -> 132 us
  local copies, waits for them, and re-layouts: 84 us -> 4.08 us
  loops' own time: 30.6 us -> 0 us
  other arithmetic: 26.3 us -> 0 us
  between operations: 14.5 us -> 0.66 us
  starting transfers between devices: 12.6 us -> 0 us
    dot_general x192 -> x0, matrix products: 316 us -> none  [matmul(): jnp.dot(left, right, precision=lax.Precision.HIGHEST, preferred_element_t...]
    psum x1 -> x0, waiting for transfers between devices: 257 us -> none  [per_device(): summed = lax.psum(probe_total, ('ty', 'tx'))]
    pallas_call x0 -> x2, Pallas kernels: none -> 132 us  [the longest x1 94.7 us: step_call(): pl.pallas_call(functools.partial(step_kernel, n_ty, n_tx), name='step', o...]
    ppermute x4 -> x0, waiting for transfers between devices: 88.9 us -> none  [passed_along(): return lax.ppermute(block, axis, route)]
    dynamic_update_slice x8 -> x0, local copies, waits for them, and re-layouts: 48.4 us -> none  [accumulate(): lax.dynamic_update_slice(gradient, previous + weight * pieces, corner)]
    another operation x1 -> x0, loops' own time: 30.6 us -> none  [per_device(): gradient, probe_total = lax.fori_loop(0, capacity, accumulate, initial)]
    dynamic_slice x20 -> x0, local copies, waits for them, and re-layouts: 15.8 us -> none  [the longest x8 8.45 us: accumulate(): previous = lax.dynamic_slice(gradient, corner, (layers, 2, patch, patch))]
    add x12 -> x0, other arithmetic: 13.2 us -> none  [the longest x4 6.61 us: accumulate(): return (gradient, probe_total + weight * probe_piece)]
  transfers between devices with their start and end apart: 5 -> 0, of which waited for: 4 -> 0; matrix products, arithmetic and copies ran while one was open for 1% -> 0% of each run, Pallas kernels for 0% -> 0%
where the time goes in v1:
time: 137 us; the launch traced here: 136 us
  Pallas kernels  132 us (96%)
  local copies, waits for them, and re-layouts  4.08 us (3%)
    pallas_call x1, Pallas kernels, step_call(): pl.pallas_call(functools.partial(step_kernel, n_ty, n_tx), name='step', o...  94.7 us
    pallas_call x1, Pallas kernels, sum_call(): pl.pallas_call(functools.partial(sum_kernel, n_ty, n_tx, scaling), name='...  37 us
    unnamed x4, local copies, waits for them, and re-layouts  4.08 us

profile of v1, /device:TPU:1, one launch (start us, length us, event | category | flops | bytes accessed | tf_op | source)
XLA Modules:
  0.0 136.4 jit_solution(11741338490034201373)
XLA Ops:
  0.6 94.7 %step.1 = (f32[2,2,384,384]{3,2,1,0:T(8,128)}, f32[2,256,256]{2,1,0:T(8,128)}) custom-call(f32[2,2,384,384]{3,2,1,0:T(8,128)} %obj.1, f32[2,256,256]{2,1,0:T(8,128)} %probe.1, f32[256,256]{1,0:T(8,128)} %phase.1, f32[4,256,256]{2,1,0:T(8,128)} %amplitude.1, s32[2,4]{1,0:T(2,128)} %offsets.1, s32[4]{0:T(128)} %live.1, ...), custom_call_target="tpu_custom_call" | custom-call | tf_op jit(solution)/shard_map/step/pallas_call | solution.py:492
  95.3 37.0 %sum_probe.1 = f32[32,16,256]{2,1,0:T(8,128)} custom-call(f32[32,16,256]{2,1,0:T(8,128)} %bitcast.3), custom_call_target="tpu_custom_call" | custom-call | tf_op jit(solution)/shard_map/sum_probe/pallas_call | solution.py:630
  132.3 0.0 copy-start
  132.3 3.3 %copy.12 = f32[2,2,384,384]{3,2,1,0:T(8,128)} copy(f32[2,2,384,384]{3,2,1,0:T(8,128)} %get-tuple-element.8) | data formatting | bytes 4718592
  135.6 0.0 copy-done
  135.6 0.8 copy.13
Async XLA Ops:
  132.3 3.3 %copy-start = (f32[32,16,256]{2,1,0:T(8,128)S(1)}, f32[32,16,256]{2,1,0:T(8,128)}, u32[]{:S(2)}) copy-start(f32[32,16,256]{2,1,0:T(8,128)} %sum_probe.1) | copy-start | bytes 1572868

commit v2 on v1

--- a/solution.py
+++ b/solution.py
@@ -118,6 +118,7 @@
 def step_kernel(
     n_ty,
     n_tx,
+    scaling,
     obj,
     probe,
     phase,
@@ -138,12 +139,21 @@
     trans,
     prop,
     target,
+    probe_part,
+    pair_part,
+    layer_part,
+    outer_part,
+    inner_chunks,
+    inner_part,
+    row_part,
     local_sem,
     get_send,
     get_recv,
     put_send,
     put_recv,
     out_sem,
+    sum_send,
+    sum_recv,
 ):
     wide = (wide_first, wide_second)
     layers, _, tile, _ = obj.shape
@@ -159,10 +169,31 @@
     up = (lax.rem(ty + n_ty - 1, n_ty), tx)
     down = (lax.rem(ty + 1, n_ty), tx)
 
+    n_row, n_outer = n_ty // 2, n_tx // INNER
+    core, row = lax.rem(ty, 2), lax.div(ty, 2)
+    inner, outer = lax.rem(tx, INNER), lax.div(tx, INNER)
+    partner = (ty + 1 - 2 * core, tx)
+
+    def outer_peer(step):
+        index = lax.rem(outer + step, n_outer)
+        return index, (ty, index * INNER + inner)
+
+    def inner_peer(step):
+        index = lax.rem(inner + step, INNER)
+        return index, (ty, outer * INNER + index)
+
+    def row_peer(step):
+        index = lax.rem(row + step, n_row)
+        return index, (index * 2 + core, tx)
+
     barrier = pltpu.get_barrier_semaphore()
-    for neighbour in (left, right, up, down):
-        pl.semaphore_signal(barrier, inc=1, device_id=neighbour, device_id_type=MESH)
-    pl.semaphore_wait(barrier, 4)
+    greeted = [left, right, up, down, partner]
+    greeted += [outer_peer(step)[1] for step in range(1, n_outer)]
+    greeted += [inner_peer(step)[1] for step in range(1, INNER)]
+    greeted += [row_peer(step)[1] for step in range(1, n_row)]
+    for device in greeted:
+        pl.semaphore_signal(barrier, inc=1, device_id=device, device_id_type=MESH)
+    pl.semaphore_wait(barrier, len(greeted))
 
     def remote(source, destination, send, recv, device):
         return pltpu.make_async_remote_copy(
@@ -205,13 +236,12 @@
             for j in range(lane_tiles)
         ]
 
-    def get_corner(s):
-        corner = pl.ds(lane_tiles, strip_tiles)
+    def get_corner(s, j):
         return get(
             s,
-            wide[s].at[:, corner, pl.ds(0, patch), :],
-            wide[s].at[:, corner, pl.ds(tile, patch), :],
-            2 * strip_tiles + lane_tiles,
+            wide[s].at[:, lane_tiles + j, pl.ds(0, patch), :],
+            wide[s].at[:, lane_tiles + j, pl.ds(tile, patch), :],
+            2 * strip_tiles + lane_tiles + j,
             up,
         )
 
@@ -220,64 +250,83 @@
             copy.start()
 
     def relay_get(s):
-        for copy in get_right(s, 0):
+        for j, copy in enumerate(get_right(s, 0)):
             copy.wait_recv()
-        get_corner(s).start()
+            get_corner(s, j).start()
 
     def finish_get(s):
-        for copy in get_right(s, 1) + get_below(s) + [get_corner(s)]:
+        for copy in get_right(s, 1) + get_below(s):
             copy.wait_recv()
+        for j in range(strip_tiles):
+            get_corner(s, j).wait_recv()
 
     def sent_get(s):
-        for copy in get_right(s, 0) + get_right(s, 1) + get_below(s) + [get_corner(s)]:
+        for copy in get_right(s, 0) + get_right(s, 1) + get_below(s):
             copy.wait_send()
+
+    def sent_corner(s):
+        for j in range(strip_tiles):
+            get_corner(s, j).wait_send()
 
     def put(s, source, destination, index, device):
         return remote(source, destination, put_send.at[s, index], put_recv.at[s, index], device)
 
-    def put_rows(s, first, size, index):
+    def put_corner(s, j):
         return put(
             s,
-            total.at[s, :, pl.ds(lane_tiles, strip_tiles), pl.ds(first, size), :],
-            from_left_tile.at[s, :, :, pl.ds(first, size), :],
-            index,
-            right,
-        )
-
-    def put_below(s, first, count, index):
+            total.at[s, :, lane_tiles + j, pl.ds(tile, patch), :],
+            from_above.at[s, :, lane_tiles + j, :, :],
+            j,
+            down,
+        )
+
+    def put_top(s, j):
         return put(
             s,
-            total.at[s, :, pl.ds(first, count), pl.ds(tile, patch), :],
-            from_above.at[s, :, pl.ds(first, count), :, :],
-            index,
+            total.at[s, :, lane_tiles + j, pl.ds(0, patch), :],
+            from_left_tile.at[s, :, j, pl.ds(0, patch), :],
+            strip_tiles + j,
+            right,
+        )
+
+    def put_bottom(s):
+        return put(
+            s,
+            total.at[s, :, pl.ds(lane_tiles, strip_tiles), pl.ds(patch, lower), :],
+            from_left_tile.at[s, :, :, pl.ds(patch, lower), :],
+            2 * strip_tiles,
+            right,
+        )
+
+    def put_below(s):
+        return put(
+            s,
+            total.at[s, :, pl.ds(0, lane_tiles), pl.ds(tile, patch), :],
+            from_above.at[s, :, pl.ds(0, lane_tiles), :, :],
+            2 * strip_tiles + 1,
             down,
         )
 
-    def put_part(s, index):
-        if index == 0:
-            return put_below(s, lane_tiles, strip_tiles, index)
-        if index == 1:
-            return put_rows(s, patch, lower, index)
-        if index == 2:
-            return put_below(s, 0, lane_tiles, index)
-        return put_rows(s, 0, patch, index)
-
     def start_put(s):
-        for index in range(3):
-            put_part(s, index).start()
+        for j in range(strip_tiles):
+            put_corner(s, j).start()
+        put_bottom(s).start()
+        put_below(s).start()
 
     def relay_put(s):
-        put_part(s, 0).wait_recv()
-
-        def add_rows(block, carry):
-            rows = pl.ds(pl.multiple_of(block * 64, 64), 64)
-            for part in range(2):
-                for j in range(lane_tiles, all_tiles):
-                    total[s, part, j, rows, :] += from_above[s, part, j, rows, :]
-            return carry
-
-        lax.fori_loop(0, patch // 64, add_rows, 0)
-        put_part(s, 3).start()
+        for j in range(strip_tiles):
+            put_corner(s, j).wait_recv()
+
+            def add_rows(block, carry):
+                rows = pl.ds(pl.multiple_of(block * 64, 64), 64)
+                for part in range(2):
+                    total[s, part, lane_tiles + j, rows, :] += from_above[
+                        s, part, lane_tiles + j, rows, :
+                    ]
+                return carry
+
+            lax.fori_loop(0, patch // 64, add_rows, 0)
+            put_top(s, j).start()
 
     def out_copies(s):
         return [
@@ -290,8 +339,10 @@
         ]
 
     def finish_put(s):
-        for index in range(1, 4):
-            put_part(s, index).wait_recv()
+        put_bottom(s).wait_recv()
+        put_below(s).wait_recv()
+        for j in range(strip_tiles):
+            put_top(s, j).wait_recv()
 
         def add_rows(block, carry):
             rows = pl.ds(pl.multiple_of(block * 64, 64), 64)
@@ -311,6 +362,134 @@
         lax.fori_loop(0, patch // 64, add_above, 0)
         for copy in out_copies(s):
             copy.start()
+
+    def summed(source, destination, index, device):
+        return remote(source, destination, sum_send.at[index], sum_recv.at[index], device)
+
+    first_outer = 1
+    first_inner = first_outer + n_outer
+    first_row = first_inner + INNER
+    second_inner = first_row + n_row
+    second_outer = second_inner + INNER
+    last_pair = second_outer + n_outer
+
+    def stage(count, peer, base, mine, source, target_of):
+        def sending(step):
+            index, device = peer(step)
+            return remote(
+                source(index),
+                target_of(mine),
+                sum_send.at[base + index],
+                sum_recv.at[base + mine],
+                device,
+            )
+
+        def receiving(step):
+            index, device = peer(step)
+            return remote(
+                source(index),
+                target_of(index),
+                sum_send.at[base + index],
+                sum_recv.at[base + index],
+                device,
+            )
+
+        def start():
+            for step in range(1, count):
+                sending(step).start()
+
+        def finish():
+            for step in range(1, count):
+                receiving(step).wait_recv()
+
+        def sent():
+            for step in range(1, count):
+                sending(step).wait_send()
+
+        return start, finish, sent
+
+    def pair_sum():
+        return summed(probe_part.at[1 - core], pair_part, 0, partner)
+
+    def pair_gather():
+        return summed(probe_grad.at[core], probe_grad.at[core], last_pair, partner)
+
+    def pair_arrival():
+        return summed(probe_grad.at[1 - core], probe_grad.at[1 - core], last_pair, partner)
+
+    outer_sum = stage(
+        n_outer, outer_peer, first_outer, outer,
+        lambda index: layer_part.at[index], lambda index: outer_part.at[index],
+    )
+    inner_sum = stage(
+        INNER, inner_peer, first_inner, inner,
+        lambda index: inner_chunks.at[index], lambda index: inner_part.at[index],
+    )
+    row_sum = stage(
+        n_row, row_peer, first_row, row,
+        lambda index: row_part.at[row], lambda index: row_part.at[index],
+    )
+    inner_gather = stage(
+        INNER, inner_peer, second_inner, inner,
+        lambda index: probe_grad.at[core, outer, inner],
+        lambda index: probe_grad.at[core, outer, index],
+    )
+    outer_gather = stage(
+        n_outer, outer_peer, second_outer, outer,
+        lambda index: probe_grad.at[core, outer],
+        lambda index: probe_grad.at[core, index],
+    )
+
+    def after_pair():
+        pair_sum().wait_recv()
+        for index in range(n_outer):
+            rows = pl.ds(index * layer_part.shape[1], layer_part.shape[1])
+            layer_part[index] = probe_part[core, rows, :] + pair_part[rows, :]
+        outer_part[outer] = layer_part[outer]
+        outer_sum[0]()
+
+    def after_outer():
+        outer_sum[1]()
+        size = inner_chunks.shape[1]
+        for index in range(INNER):
+            rows = pl.ds(index * size, size)
+            value = outer_part[0, rows, :]
+            for other in range(1, n_outer):
+                value += outer_part[other, rows, :]
+            inner_chunks[index] = value
+        inner_part[inner] = inner_chunks[inner]
+        inner_sum[0]()
+
+    def after_inner():
+        inner_sum[1]()
+        value = inner_part[0]
+        for index in range(1, INNER):
+            value += inner_part[index]
+        row_part[row] = value
+        row_sum[0]()
+
+    def after_row():
+        row_sum[1]()
+        value = row_part[0]
+        for index in range(1, n_row):
+            value += row_part[index]
+        probe_grad[core, outer, inner] = value * scaling
+        inner_gather[0]()
+
+    def after_inner_gather():
+        inner_gather[1]()
+        outer_gather[0]()
+
+    def after_outer_gather():
+        outer_gather[1]()
+        pair_gather().start()
+
+    def finish_sum():
+        pair_arrival().wait_recv()
+        pair_gather().wait_send()
+        pair_sum().wait_send()
+        for part in (outer_sum, inner_sum, row_sum, inner_gather, outer_gather):
+            part[2]()
 
     start_get(0)
     local = [
@@ -343,9 +522,9 @@
     for copy in local:
         copy.wait()
     relay_get(0)
-    finish_get(0)
     sent_get(0)
     start_get(1)
+    finish_get(0)
 
     lane = lax.broadcasted_iota(jnp.int32, (patch, LANES), 1)
 
@@ -414,9 +593,11 @@
         return carry
 
     lax.fori_loop(0, slots, first_layer, 0)
+    sent_corner(0)
     relay_get(1)
+    sent_get(1)
     finish_get(1)
-    sent_get(1)
+    sent_corner(1)
 
     def second_layer(q, carry):
         trans_real, trans_imag = window(1, 0, q), window(1, 1, q)
@@ -439,16 +620,16 @@
 
     lax.fori_loop(0, slots, second_layer, 0)
     strip = range(lane_tiles, all_tiles)
-    inner = range(lane_tiles)
+    own = range(lane_tiles)
 
     def send_edges(s):
         gather(s, strip, 0, tile + patch)
-        gather(s, inner, tile, patch)
+        gather(s, own, tile, patch)
         start_put(s)
-        gather(s, inner, 0, tile)
 
     send_edges(1)
-    probe_grad[...] = jnp.zeros(probe_grad.shape, F32)
+    gather(1, own, 0, tile)
+    probe_part[...] = jnp.zeros(probe_part.shape, F32)
 
     def third_layer(q, carry):
         freq_real, freq_imag = forward(psi[q, 0], psi[q, 1], tables)
@@ -460,41 +641,58 @@
         deposit(q, 0, probe[0] * back_real + probe[1] * back_imag)
         deposit(q, 1, probe[0] * back_imag - probe[1] * back_real)
         weight = live[q].astype(F32)
-        probe_grad[0] += weight * (trans[q, 0] * back_real + trans[q, 1] * back_imag)
-        probe_grad[1] += weight * (trans[q, 0] * back_imag - trans[q, 1] * back_real)
+        probe_part[0] += weight * (trans[q, 0] * back_real + trans[q, 1] * back_imag)
+        probe_part[1] += weight * (trans[q, 0] * back_imag - trans[q, 1] * back_real)
         return carry
 
     lax.fori_loop(0, slots // 2, third_layer, 0)
     relay_put(1)
     lax.fori_loop(slots // 2, slots, third_layer, 0)
+    pair_sum().start()
     send_edges(0)
+    after_pair()
+    gather(0, own, 0, tile)
     finish_put(1)
+    after_outer()
     relay_put(0)
+    after_inner()
+    after_row()
+    after_inner_gather()
+    after_outer_gather()
     finish_put(0)
+    finish_sum()
     for s in range(layers):
-        for index in range(4):
-            put_part(s, index).wait_send()
+        put_bottom(s).wait_send()
+        put_below(s).wait_send()
+        for j in range(strip_tiles):
+            put_corner(s, j).wait_send()
+            put_top(s, j).wait_send()
         for copy in out_copies(s):
             copy.wait()
 
 
-def step_call(n_ty, n_tx, *operands):
+def step_call(n_ty, n_tx, scaling, *operands):
     obj, probe, _, amplitude, _, _, _, _ = operands
     layers, _, tile, _ = obj.shape
     patch = probe.shape[1]
     slots = amplitude.shape[0]
     lane_tiles, strip_tiles = tile // LANES, patch // LANES
     all_tiles = lane_tiles + strip_tiles
-    gets = 2 * strip_tiles + lane_tiles + 1
+    gets = 3 * strip_tiles + lane_tiles
+    puts = 2 * strip_tiles + 2
+    n_row, n_outer = n_ty // 2, n_tx // INNER
+    layer_rows = patch // n_outer
+    chunk = layer_rows // INNER
+    sums = 2 * n_outer + 2 * INNER + n_row + 2
     vmem = pl.BlockSpec(memory_space=pltpu.VMEM)
     smem = pl.BlockSpec(memory_space=pltpu.SMEM)
     whole = pl.BlockSpec(memory_space=pl.ANY)
     return pl.pallas_call(
-        functools.partial(step_kernel, n_ty, n_tx),
+        functools.partial(step_kernel, n_ty, n_tx, scaling),
         name="step",
         out_shape=(
             jax.ShapeDtypeStruct(obj.shape, F32),
-            jax.ShapeDtypeStruct(probe.shape, F32),
+            jax.ShapeDtypeStruct((2, n_outer, INNER, chunk, patch), F32),
         ),
         in_specs=[whole, vmem, vmem, vmem, smem, smem, vmem, vmem],
         out_specs=(whole, vmem),
@@ -509,12 +707,21 @@
             pltpu.VMEM((slots, 2, patch, patch), F32),
             pltpu.VMEM((2, patch, patch), F32),
             pltpu.VMEM((slots, patch, patch), F32),
+            pltpu.VMEM((2, patch, patch), F32),
+            pltpu.VMEM((patch, patch), F32),
+            pltpu.VMEM((n_outer, layer_rows, patch), F32),
+            pltpu.VMEM((n_outer, layer_rows, patch), F32),
+            pltpu.VMEM((INNER, chunk, patch), F32),
+            pltpu.VMEM((INNER, chunk, patch), F32),
+            pltpu.VMEM((n_row, chunk, patch), F32),
             pltpu.SemaphoreType.DMA((layers, lane_tiles)),
             pltpu.SemaphoreType.DMA((layers, gets)),
             pltpu.SemaphoreType.DMA((layers, gets)),
-            pltpu.SemaphoreType.DMA((layers, 4)),
-            pltpu.SemaphoreType.DMA((layers, 4)),
+            pltpu.SemaphoreType.DMA((layers, puts)),
+            pltpu.SemaphoreType.DMA((layers, puts)),
             pltpu.SemaphoreType.DMA((layers, lane_tiles)),
+            pltpu.SemaphoreType.DMA((sums,)),
+            pltpu.SemaphoreType.DMA((sums,)),
         ],
         compiler_params=pltpu.CompilerParams(
             collective_id=0, has_side_effects=True, vmem_limit_bytes=60 * 1024 * 1024
@@ -522,140 +729,16 @@
     )(*operands)
 
 
-def sum_kernel(
-    n_ty, n_tx, scaling, part, whole, near, far, near_send, near_recv, far_send, far_recv,
-    last_send, last_recv,
-):
-    near_count, far_count = n_ty * INNER, n_tx // INNER
-    ty, tx = lax.axis_index("ty"), lax.axis_index("tx")
-    inner, outer = lax.rem(tx, INNER), lax.div(tx, INNER)
-    mine = ty * INNER + inner
-
-    def near_peer(step):
-        index = lax.rem(mine + step, near_count)
-        return index, (lax.div(index, INNER), outer * INNER + lax.rem(index, INNER))
-
-    def far_peer(step):
-        index = lax.rem(outer + step, far_count)
-        return index, (ty, index * INNER + inner)
-
-    barrier = pltpu.get_barrier_semaphore()
-
-    def greet_near(step, carry):
-        pl.semaphore_signal(barrier, inc=1, device_id=near_peer(step)[1], device_id_type=MESH)
-        return carry
-
-    def greet_far(step, carry):
-        pl.semaphore_signal(barrier, inc=1, device_id=far_peer(step)[1], device_id_type=MESH)
-        return carry
-
-    lax.fori_loop(1, near_count, greet_near, 0)
-    lax.fori_loop(1, far_count, greet_far, 0)
-    pl.semaphore_wait(barrier, near_count + far_count - 2)
-
-    def remote(source, destination, send, recv, device):
-        return pltpu.make_async_remote_copy(
-            src_ref=source,
-            dst_ref=destination,
-            send_sem=send,
-            recv_sem=recv,
-            device_id=device,
-            device_id_type=MESH,
-        )
-
-    def exchange(count, peer, make):
-        def start(step, carry):
-            make(*peer(step))[0].start()
-            return carry
-
-        def wait(step, carry):
-            make(*peer(step))[1].wait_recv()
-            return carry
-
-        def sent(step, carry):
-            make(*peer(step))[0].wait_send()
-            return carry
-
-        lax.fori_loop(1, count, start, 0)
-        lax.fori_loop(1, count, wait, 0)
-        return lambda: lax.fori_loop(1, count, sent, 0)
-
-    def scatter(index, device):
-        return (
-            remote(part.at[index], near.at[mine], near_send.at[index], near_recv.at[mine], device),
-            remote(part.at[mine], near.at[index], near_send.at[index], near_recv.at[index], device),
-        )
-
-    near[mine] = part[mine]
-    done_near = exchange(near_count, near_peer, scatter)
-    value = near[0]
-    for index in range(1, near_count):
-        value += near[index]
-    far[outer] = value
-
-    def across(index, device):
-        return (
-            remote(far.at[outer], far.at[outer], far_send.at[index], far_recv.at[outer], device),
-            remote(far.at[outer], far.at[index], far_send.at[index], far_recv.at[index], device),
-        )
-
-    done_far = exchange(far_count, far_peer, across)
-    value = far[0]
-    for index in range(1, far_count):
-        value += far[index]
-    whole[mine] = value * scaling
-
-    def spread(index, device):
-        return (
-            remote(
-                whole.at[mine], whole.at[mine], last_send.at[index], last_recv.at[mine], device
-            ),
-            remote(
-                whole.at[mine], whole.at[index], last_send.at[index], last_recv.at[index], device
-            ),
-        )
-
-    done_last = exchange(near_count, near_peer, spread)
-    done_near()
-    done_far()
-    done_last()
-
-
-def sum_call(n_ty, n_tx, scaling, value):
-    near_count, far_count = n_ty * INNER, n_tx // INNER
-    width = value.shape[-1]
-    rows = value.size // width // near_count
-    vmem = pl.BlockSpec(memory_space=pltpu.VMEM)
-    sems = pltpu.SemaphoreType.DMA
-    summed = pl.pallas_call(
-        functools.partial(sum_kernel, n_ty, n_tx, scaling),
-        name="sum_probe",
-        out_shape=jax.ShapeDtypeStruct((near_count, rows, width), F32),
-        in_specs=[vmem],
-        out_specs=vmem,
-        scratch_shapes=[
-            pltpu.VMEM((near_count, rows, width), F32),
-            pltpu.VMEM((far_count, rows, width), F32),
-            sems((near_count,)),
-            sems((near_count,)),
-            sems((far_count,)),
-            sems((far_count,)),
-            sems((near_count,)),
-            sems((near_count,)),
-        ],
-        compiler_params=pltpu.CompilerParams(collective_id=1, has_side_effects=True),
-    )(value.reshape(near_count, rows, width))
-    return summed.reshape(value.shape)
-
-
 def solution(mesh):
     n_ty, n_tx = mesh.shape["ty"], mesh.shape["tx"]
 
     def per_device(object_field, probe_wave, prop_phase, amplitude, offsets, live_slots):
         patch = probe_wave.shape[1]
-        owned, probe_part = step_call(
+        scaling = 1.0 / math.sqrt(live_slots.shape[0] * n_ty * n_tx)
+        owned, shared = step_call(
             n_ty,
             n_tx,
+            scaling,
             object_field,
             probe_wave,
             prop_phase,
@@ -665,8 +748,7 @@
             jnp.asarray(dft_halves(patch)),
             jnp.asarray(even_odd(patch)),
         )
-        scaling = 1.0 / math.sqrt(live_slots.shape[0] * n_ty * n_tx)
-        return owned, sum_call(n_ty, n_tx, scaling, probe_part)
+        return owned, shared.reshape(probe_wave.shape)
 
     placed = (
         P(None, None, "ty", "tx"),

time: 137 us -> 120 us (0.88)
  Pallas kernels: 132 us -> 113 us
    pallas_call x2 -> x1, Pallas kernels: 132 us -> 113 us  [step_call(): pl.pallas_call(functools.partial(step_kernel, n_ty, n_tx, scaling), name=...]
where the time goes in v2:
time: 120 us; the launch traced here: 118 us
  Pallas kernels  113 us (94%)
  local copies, waits for them, and re-layouts  4.08 us (3%)
    pallas_call x1, Pallas kernels, step_call(): pl.pallas_call(functools.partial(step_kernel, n_ty, n_tx, scaling), name=...  113 us
    unnamed x4, local copies, waits for them, and re-layouts  4.08 us

profile of v2, /device:TPU:1, one launch (start us, length us, event | category | flops | bytes accessed | tf_op | source)
XLA Modules:
  0.0 118.1 jit_solution(17557049276532933430)
XLA Ops:
  0.6 113.4 %step.1 = (f32[2,2,384,384]{3,2,1,0:T(8,128)}, f32[2,8,4,8,256]{4,3,2,1,0:T(8,128)}) custom-call(f32[2,2,384,384]{3,2,1,0:T(8,128)} %obj.1, f32[2,256,256]{2,1,0:T(8,128)} %probe.1, f32[256,256]{1,0:T(8,128)} %phase.1, f32[4,256,256]{2,1,0:T(8,128)} %amplitude.1, s32[2,4]{1,0:T(2,128)} %offsets.1, s32[4]{0:T(128)} %live.1, ...), custom_call_target="tpu_custom_call" | custom-call | tf_op jit(solution)/shard_map/step/pallas_call | solution.py:690
  114.0 0.0 copy-start
  114.0 3.3 %copy.12 = f32[2,2,384,384]{3,2,1,0:T(8,128)} copy(f32[2,2,384,384]{3,2,1,0:T(8,128)} %get-tuple-element.8) | data formatting | bytes 4718592
  117.3 0.0 copy-done
  117.3 0.8 copy.13
Async XLA Ops:
  114.0 3.3 %copy-start = (f32[2,8,4,8,256]{4,3,2,1,0:T(8,128)S(1)}, f32[2,8,4,8,256]{4,3,2,1,0:T(8,128)}, u32[]{:S(2)}) copy-start(f32[2,8,4,8,256]{4,3,2,1,0:T(8,128)} %get-tuple-element.5) | copy-start | bytes 1572868

commit v3 on v2

--- a/solution.py
+++ b/solution.py
@@ -131,7 +131,8 @@
     probe_grad,
     wide_first,
     wide_second,
-    padded,
+    padded_first,
+    padded_second,
     total,
     from_left_tile,
     from_above,
@@ -143,7 +144,6 @@
     pair_part,
     layer_part,
     outer_part,
-    inner_chunks,
     inner_part,
     row_part,
     local_sem,
@@ -156,6 +156,7 @@
     sum_recv,
 ):
     wide = (wide_first, wide_second)
+    padded = (padded_first, padded_second)
     layers, _, tile, _ = obj.shape
     patch = probe.shape[1]
     slots = amplitude.shape[0]
@@ -307,26 +308,23 @@
             down,
         )
 
-    def start_put(s):
+    def start_corners(s):
         for j in range(strip_tiles):
             put_corner(s, j).start()
-        put_bottom(s).start()
-        put_below(s).start()
-
-    def relay_put(s):
-        for j in range(strip_tiles):
-            put_corner(s, j).wait_recv()
-
-            def add_rows(block, carry):
-                rows = pl.ds(pl.multiple_of(block * 64, 64), 64)
-                for part in range(2):
-                    total[s, part, lane_tiles + j, rows, :] += from_above[
-                        s, part, lane_tiles + j, rows, :
-                    ]
-                return carry
-
-            lax.fori_loop(0, patch // 64, add_rows, 0)
-            put_top(s, j).start()
+
+    def relay_put(s, j):
+        put_corner(s, j).wait_recv()
+
+        def add_rows(block, carry):
+            rows = pl.ds(pl.multiple_of(block * 64, 64), 64)
+            for part in range(2):
+                total[s, part, lane_tiles + j, rows, :] += from_above[
+                    s, part, lane_tiles + j, rows, :
+                ]
+            return carry
+
+        lax.fori_loop(0, patch // 64, add_rows, 0)
+        put_top(s, j).start()
 
     def out_copies(s):
         return [
@@ -369,8 +367,7 @@
     first_outer = 1
     first_inner = first_outer + n_outer
     first_row = first_inner + INNER
-    second_inner = first_row + n_row
-    second_outer = second_inner + INNER
+    second_outer = first_row + n_row
     last_pair = second_outer + n_outer
 
     def stage(count, peer, base, mine, source, target_of):
@@ -423,16 +420,11 @@
     )
     inner_sum = stage(
         INNER, inner_peer, first_inner, inner,
-        lambda index: inner_chunks.at[index], lambda index: inner_part.at[index],
+        lambda index: inner_part.at[inner], lambda index: inner_part.at[index],
     )
     row_sum = stage(
         n_row, row_peer, first_row, row,
         lambda index: row_part.at[row], lambda index: row_part.at[index],
-    )
-    inner_gather = stage(
-        INNER, inner_peer, second_inner, inner,
-        lambda index: probe_grad.at[core, outer, inner],
-        lambda index: probe_grad.at[core, outer, index],
     )
     outer_gather = stage(
         n_outer, outer_peer, second_outer, outer,
@@ -448,36 +440,25 @@
         outer_part[outer] = layer_part[outer]
         outer_sum[0]()
 
+    def reduced(parts, count):
+        value = parts[0]
+        for index in range(1, count):
+            value += parts[index]
+        return value
+
     def after_outer():
         outer_sum[1]()
-        size = inner_chunks.shape[1]
-        for index in range(INNER):
-            rows = pl.ds(index * size, size)
-            value = outer_part[0, rows, :]
-            for other in range(1, n_outer):
-                value += outer_part[other, rows, :]
-            inner_chunks[index] = value
-        inner_part[inner] = inner_chunks[inner]
+        inner_part[inner] = reduced(outer_part, n_outer)
         inner_sum[0]()
 
     def after_inner():
         inner_sum[1]()
-        value = inner_part[0]
-        for index in range(1, INNER):
-            value += inner_part[index]
-        row_part[row] = value
+        row_part[row] = reduced(inner_part, INNER)
         row_sum[0]()
 
     def after_row():
         row_sum[1]()
-        value = row_part[0]
-        for index in range(1, n_row):
-            value += row_part[index]
-        probe_grad[core, outer, inner] = value * scaling
-        inner_gather[0]()
-
-    def after_inner_gather():
-        inner_gather[1]()
+        probe_grad[core, outer] = reduced(row_part, n_row) * scaling
         outer_gather[0]()
 
     def after_outer_gather():
@@ -488,7 +469,7 @@
         pair_arrival().wait_recv()
         pair_gather().wait_send()
         pair_sum().wait_send()
-        for part in (outer_sum, inner_sum, row_sum, inner_gather, outer_gather):
+        for part in (outer_sum, inner_sum, row_sum, outer_gather):
             part[2]()
 
     start_get(0)
@@ -503,10 +484,12 @@
         copy.start()
 
     def clear(q, carry):
-        for part in range(2):
-            for j in range(strip_tiles + 1):
-                padded[q, part, j, pl.ds(0, tile), :] = jnp.zeros((tile, LANES), F32)
-                padded[q, part, j, pl.ds(tile + patch, tile), :] = jnp.zeros((tile, LANES), F32)
+        margin = jnp.zeros((tile, LANES), F32)
+        for s in range(layers):
+            for part in range(2):
+                for j in range(strip_tiles + 1):
+                    padded[s][q, part, j, pl.ds(0, tile), :] = margin
+                    padded[s][q, part, j, pl.ds(tile + patch, tile), :] = margin
         return carry
 
     lax.fori_loop(0, slots, clear, 0)
@@ -544,7 +527,7 @@
             [jnp.where(keep, rolled[k], rolled[k + 1]) for k in range(strip_tiles)], axis=1
         )
 
-    def deposit(q, part, piece):
+    def deposit(s, q, part, piece):
         _, _, shift = place(q)
         rolled = [
             pltpu.roll(piece[:, k * LANES : (k + 1) * LANES], shift, 1) for k in range(strip_tiles)
@@ -552,7 +535,7 @@
         rolled = [jnp.zeros((patch, LANES), F32)] + rolled + [jnp.zeros((patch, LANES), F32)]
         keep = lane >= shift
         for k in range(strip_tiles + 1):
-            padded[q, part, k, pl.ds(tile, patch), :] = jnp.where(keep, rolled[k + 1], rolled[k])
+            padded[s][q, part, k, pl.ds(tile, patch), :] = jnp.where(keep, rolled[k + 1], rolled[k])
 
     def gather(s, tiles, first, size):
         places = [place(q) for q in range(slots)]
@@ -571,7 +554,7 @@
                     value = jnp.zeros((64, LANES), F32)
                     for q in range(slots):
                         rows = pl.ds(tile - places[q][0] + begin, 64)
-                        value += weights[q] * padded[q, part, sources[q], rows, :]
+                        value += weights[q] * padded[s][q, part, sources[q], rows, :]
                     total[s, part, j, pl.ds(pl.multiple_of(begin, 64), 64), :] = value
             return carry
 
@@ -611,8 +594,8 @@
         factor = target[q] / jnp.sqrt(energy) - 1.0
         back_real, back_imag = backward(freq_real * factor, freq_imag * factor, tables)
         wave_real, wave_imag = psi[q, 0], psi[q, 1]
-        deposit(q, 0, wave_real * back_real + wave_imag * back_imag)
-        deposit(q, 1, wave_real * back_imag - wave_imag * back_real)
+        deposit(1, q, 0, wave_real * back_real + wave_imag * back_imag)
+        deposit(1, q, 1, wave_real * back_imag - wave_imag * back_real)
         trans_real, trans_imag = window(1, 0, q), window(1, 1, q)
         psi[q, 0] = trans_real * back_real + trans_imag * back_imag
         psi[q, 1] = trans_real * back_imag - trans_imag * back_real
@@ -622,13 +605,10 @@
     strip = range(lane_tiles, all_tiles)
     own = range(lane_tiles)
 
-    def send_edges(s):
-        gather(s, strip, 0, tile + patch)
-        gather(s, own, tile, patch)
-        start_put(s)
-
-    send_edges(1)
-    gather(1, own, 0, tile)
+    gather(1, strip, 0, tile + patch)
+    start_corners(1)
+    put_bottom(1).start()
+    gather(1, own, tile, patch)
     probe_part[...] = jnp.zeros(probe_part.shape, F32)
 
     def third_layer(q, carry):
@@ -638,26 +618,32 @@
             prop[0] * freq_imag - prop[1] * freq_real,
             tables,
         )
-        deposit(q, 0, probe[0] * back_real + probe[1] * back_imag)
-        deposit(q, 1, probe[0] * back_imag - probe[1] * back_real)
+        deposit(0, q, 0, probe[0] * back_real + probe[1] * back_imag)
+        deposit(0, q, 1, probe[0] * back_imag - probe[1] * back_real)
         weight = live[q].astype(F32)
         probe_part[0] += weight * (trans[q, 0] * back_real + trans[q, 1] * back_imag)
         probe_part[1] += weight * (trans[q, 0] * back_imag - trans[q, 1] * back_real)
         return carry
 
-    lax.fori_loop(0, slots // 2, third_layer, 0)
-    relay_put(1)
-    lax.fori_loop(slots // 2, slots, third_layer, 0)
+    lax.fori_loop(0, slots, third_layer, 0)
     pair_sum().start()
-    send_edges(0)
+    for j in range(strip_tiles):
+        relay_put(1, j)
     after_pair()
+    put_below(1).start()
+    gather(0, strip, 0, tile + patch)
+    start_corners(0)
+    gather(0, own, tile, patch)
+    gather(1, own, 0, tile)
+    after_outer()
+    put_bottom(0).start()
     gather(0, own, 0, tile)
+    after_inner()
+    relay_put(0, 0)
+    after_row()
+    relay_put(0, 1)
+    put_below(0).start()
     finish_put(1)
-    after_outer()
-    relay_put(0)
-    after_inner()
-    after_row()
-    after_inner_gather()
     after_outer_gather()
     finish_put(0)
     finish_sum()
@@ -682,8 +668,7 @@
     puts = 2 * strip_tiles + 2
     n_row, n_outer = n_ty // 2, n_tx // INNER
     layer_rows = patch // n_outer
-    chunk = layer_rows // INNER
-    sums = 2 * n_outer + 2 * INNER + n_row + 2
+    sums = 2 * n_outer + INNER + n_row + 2
     vmem = pl.BlockSpec(memory_space=pltpu.VMEM)
     smem = pl.BlockSpec(memory_space=pltpu.SMEM)
     whole = pl.BlockSpec(memory_space=pl.ANY)
@@ -692,13 +677,14 @@
         name="step",
         out_shape=(
             jax.ShapeDtypeStruct(obj.shape, F32),
-            jax.ShapeDtypeStruct((2, n_outer, INNER, chunk, patch), F32),
+            jax.ShapeDtypeStruct((2, n_outer, layer_rows, patch), F32),
         ),
         in_specs=[whole, vmem, vmem, vmem, smem, smem, vmem, vmem],
         out_specs=(whole, vmem),
         scratch_shapes=[
             pltpu.VMEM((2, all_tiles, tile + patch, LANES), F32),
             pltpu.VMEM((2, all_tiles, tile + patch, LANES), F32),
+            pltpu.VMEM((slots, 2, strip_tiles + 1, 2 * tile + patch, LANES), F32),
             pltpu.VMEM((slots, 2, strip_tiles + 1, 2 * tile + patch, LANES), F32),
             pltpu.VMEM((layers, 2, all_tiles, tile + patch, LANES), F32),
             pltpu.VMEM((layers, 2, strip_tiles, tile, LANES), F32),
@@ -711,9 +697,8 @@
             pltpu.VMEM((patch, patch), F32),
             pltpu.VMEM((n_outer, layer_rows, patch), F32),
             pltpu.VMEM((n_outer, layer_rows, patch), F32),
-            pltpu.VMEM((INNER, chunk, patch), F32),
-            pltpu.VMEM((INNER, chunk, patch), F32),
-            pltpu.VMEM((n_row, chunk, patch), F32),
+            pltpu.VMEM((INNER, layer_rows, patch), F32),
+            pltpu.VMEM((n_row, layer_rows, patch), F32),
             pltpu.SemaphoreType.DMA((layers, lane_tiles)),
             pltpu.SemaphoreType.DMA((layers, gets)),
             pltpu.SemaphoreType.DMA((layers, gets)),

time: 120 us -> 118 us (0.983); the launches traced: 118 us -> 117 us
  no operation moved by 1% of the time
where the time goes in v3:
time: 118 us; the launch traced here: 117 us
  Pallas kernels  113 us (96%)
  local copies, waits for them, and re-layouts  4.08 us (3%)
    pallas_call x1, Pallas kernels, step_call(): pl.pallas_call(functools.partial(step_kernel, n_ty, n_tx, scaling), name=...  113 us
    unnamed x4, local copies, waits for them, and re-layouts  4.08 us

profile of v3, /device:TPU:1, one launch (start us, length us, event | category | flops | bytes accessed | tf_op | source)
XLA Modules:
  0.0 117.4 jit_solution(1456419047762636527)
XLA Ops:
  0.6 112.6 %step.1 = (f32[2,2,384,384]{3,2,1,0:T(8,128)}, f32[2,8,32,256]{3,2,1,0:T(8,128)}) custom-call(f32[2,2,384,384]{3,2,1,0:T(8,128)} %obj.1, f32[2,256,256]{2,1,0:T(8,128)} %probe.1, f32[256,256]{1,0:T(8,128)} %phase.1, f32[4,256,256]{2,1,0:T(8,128)} %amplitude.1, s32[2,4]{1,0:T(2,128)} %offsets.1, s32[4]{0:T(128)} %live.1, ...), custom_call_target="tpu_custom_call" | custom-call | tf_op jit(solution)/shard_map/step/pallas_call | solution.py:675
  113.3 0.0 copy-start
  113.3 3.3 %copy.12 = f32[2,2,384,384]{3,2,1,0:T(8,128)} copy(f32[2,2,384,384]{3,2,1,0:T(8,128)} %get-tuple-element.8) | data formatting | bytes 4718592
  116.6 0.0 copy-done
  116.6 0.8 copy.13
Async XLA Ops:
  113.3 3.3 %copy-start = (f32[2,8,32,256]{3,2,1,0:T(8,128)S(1)}, f32[2,8,32,256]{3,2,1,0:T(8,128)}, u32[]{:S(2)}) copy-start(f32[2,8,32,256]{3,2,1,0:T(8,128)} %get-tuple-element.5) | copy-start | bytes 1572868

commit v4 on v3

--- a/solution.py
+++ b/solution.py
@@ -142,10 +142,11 @@
     target,
     probe_part,
     pair_part,
-    layer_part,
+    pair_sums,
+    row_part,
+    row_sums,
     outer_part,
     inner_part,
-    row_part,
     local_sem,
     get_send,
     get_recv,
@@ -312,7 +313,7 @@
         for j in range(strip_tiles):
             put_corner(s, j).start()
 
-    def relay_put(s, j):
+    def add_corner(s, j):
         put_corner(s, j).wait_recv()
 
         def add_rows(block, carry):
@@ -324,7 +325,6 @@
             return carry
 
         lax.fori_loop(0, patch // 64, add_rows, 0)
-        put_top(s, j).start()
 
     def out_copies(s):
         return [
@@ -364,11 +364,12 @@
     def summed(source, destination, index, device):
         return remote(source, destination, sum_send.at[index], sum_recv.at[index], device)
 
-    first_outer = 1
+    first_row = 1
+    first_outer = first_row + n_row
     first_inner = first_outer + n_outer
-    first_row = first_inner + INNER
-    second_outer = first_row + n_row
-    last_pair = second_outer + n_outer
+    second_outer = first_inner + INNER
+    second_row = second_outer + n_outer
+    last_pair = second_row + n_row
 
     def stage(count, peer, base, mine, source, target_of):
         def sending(step):
@@ -414,31 +415,28 @@
     def pair_arrival():
         return summed(probe_grad.at[1 - core], probe_grad.at[1 - core], last_pair, partner)
 
+    row_sum = stage(
+        n_row, row_peer, first_row, row,
+        lambda index: pair_sums.at[index], lambda index: row_part.at[index],
+    )
     outer_sum = stage(
         n_outer, outer_peer, first_outer, outer,
-        lambda index: layer_part.at[index], lambda index: outer_part.at[index],
+        lambda index: row_sums.at[index], lambda index: outer_part.at[index],
     )
     inner_sum = stage(
         INNER, inner_peer, first_inner, inner,
         lambda index: inner_part.at[inner], lambda index: inner_part.at[index],
     )
-    row_sum = stage(
-        n_row, row_peer, first_row, row,
-        lambda index: row_part.at[row], lambda index: row_part.at[index],
-    )
     outer_gather = stage(
         n_outer, outer_peer, second_outer, outer,
-        lambda index: probe_grad.at[core, outer],
+        lambda index: probe_grad.at[core, row, outer],
+        lambda index: probe_grad.at[core, row, index],
+    )
+    row_gather = stage(
+        n_row, row_peer, second_row, row,
+        lambda index: probe_grad.at[core, row],
         lambda index: probe_grad.at[core, index],
     )
-
-    def after_pair():
-        pair_sum().wait_recv()
-        for index in range(n_outer):
-            rows = pl.ds(index * layer_part.shape[1], layer_part.shape[1])
-            layer_part[index] = probe_part[core, rows, :] + pair_part[rows, :]
-        outer_part[outer] = layer_part[outer]
-        outer_sum[0]()
 
     def reduced(parts, count):
         value = parts[0]
@@ -446,6 +444,27 @@
             value += parts[index]
         return value
 
+    def after_pair():
+        pair_sum().wait_recv()
+        size = pair_sums.shape[1]
+        for index in range(n_row):
+            rows = pl.ds(index * size, size)
+            pair_sums[index] = probe_part[core, rows, :] + pair_part[rows, :]
+        row_part[row] = pair_sums[row]
+        row_sum[0]()
+
+    def after_row():
+        row_sum[1]()
+        size = row_sums.shape[1]
+        for index in range(n_outer):
+            rows = pl.ds(index * size, size)
+            value = row_part[0, rows, :]
+            for other in range(1, n_row):
+                value += row_part[other, rows, :]
+            row_sums[index] = value
+        outer_part[outer] = row_sums[outer]
+        outer_sum[0]()
+
     def after_outer():
         outer_sum[1]()
         inner_part[inner] = reduced(outer_part, n_outer)
@@ -453,23 +472,22 @@
 
     def after_inner():
         inner_sum[1]()
-        row_part[row] = reduced(inner_part, INNER)
-        row_sum[0]()
-
-    def after_row():
-        row_sum[1]()
-        probe_grad[core, outer] = reduced(row_part, n_row) * scaling
+        probe_grad[core, row, outer] = reduced(inner_part, INNER) * scaling
         outer_gather[0]()
 
     def after_outer_gather():
         outer_gather[1]()
+        row_gather[0]()
+
+    def after_row_gather():
+        row_gather[1]()
         pair_gather().start()
 
     def finish_sum():
         pair_arrival().wait_recv()
         pair_gather().wait_send()
         pair_sum().wait_send()
-        for part in (outer_sum, inner_sum, row_sum, outer_gather):
+        for part in (row_sum, outer_sum, inner_sum, outer_gather, row_gather):
             part[2]()
 
     start_get(0)
@@ -601,7 +619,8 @@
         psi[q, 1] = trans_real * back_imag - trans_imag * back_real
         return carry
 
-    lax.fori_loop(0, slots, second_layer, 0)
+    for q in range(slots):
+        second_layer(q, 0)
     strip = range(lane_tiles, all_tiles)
     own = range(lane_tiles)
 
@@ -625,26 +644,32 @@
         probe_part[1] += weight * (trans[q, 0] * back_imag - trans[q, 1] * back_real)
         return carry
 
-    lax.fori_loop(0, slots, third_layer, 0)
+    for q in range(slots):
+        third_layer(q, 0)
     pair_sum().start()
     for j in range(strip_tiles):
-        relay_put(1, j)
+        add_corner(1, j)
     after_pair()
-    put_below(1).start()
+    put_top(1, 0).start()
     gather(0, strip, 0, tile + patch)
     start_corners(0)
+    put_below(1).start()
     gather(0, own, tile, patch)
     gather(1, own, 0, tile)
+    after_row()
+    put_top(1, 1).start()
+    gather(0, own, 0, tile)
     after_outer()
     put_bottom(0).start()
-    gather(0, own, 0, tile)
+    add_corner(0, 0)
     after_inner()
-    relay_put(0, 0)
-    after_row()
-    relay_put(0, 1)
+    put_top(0, 0).start()
+    add_corner(0, 1)
+    after_outer_gather()
+    put_top(0, 1).start()
     put_below(0).start()
     finish_put(1)
-    after_outer_gather()
+    after_row_gather()
     finish_put(0)
     finish_sum()
     for s in range(layers):
@@ -667,8 +692,9 @@
     gets = 3 * strip_tiles + lane_tiles
     puts = 2 * strip_tiles + 2
     n_row, n_outer = n_ty // 2, n_tx // INNER
-    layer_rows = patch // n_outer
-    sums = 2 * n_outer + INNER + n_row + 2
+    row_rows = patch // n_row
+    chunk = row_rows // n_outer
+    sums = 2 * n_row + 2 * n_outer + INNER + 2
     vmem = pl.BlockSpec(memory_space=pltpu.VMEM)
     smem = pl.BlockSpec(memory_space=pltpu.SMEM)
     whole = pl.BlockSpec(memory_space=pl.ANY)
@@ -677,7 +703,7 @@
         name="step",
         out_shape=(
             jax.ShapeDtypeStruct(obj.shape, F32),
-            jax.ShapeDtypeStruct((2, n_outer, layer_rows, patch), F32),
+            jax.ShapeDtypeStruct((2, n_row, n_outer, chunk, patch), F32),
         ),
         in_specs=[whole, vmem, vmem, vmem, smem, smem, vmem, vmem],
         out_specs=(whole, vmem),
@@ -695,10 +721,11 @@
             pltpu.VMEM((slots, patch, patch), F32),
             pltpu.VMEM((2, patch, patch), F32),
             pltpu.VMEM((patch, patch), F32),
-            pltpu.VMEM((n_outer, layer_rows, patch), F32),
-            pltpu.VMEM((n_outer, layer_rows, patch), F32),
-            pltpu.VMEM((INNER, layer_rows, patch), F32),
-            pltpu.VMEM((n_row, layer_rows, patch), F32),
+            pltpu.VMEM((n_row, row_rows, patch), F32),
+            pltpu.VMEM((n_row, row_rows, patch), F32),
+            pltpu.VMEM((n_outer, chunk, patch), F32),
+            pltpu.VMEM((n_outer, chunk, patch), F32),
+            pltpu.VMEM((INNER, chunk, patch), F32),
             pltpu.SemaphoreType.DMA((layers, lane_tiles)),
             pltpu.SemaphoreType.DMA((layers, gets)),
             pltpu.SemaphoreType.DMA((layers, gets)),

time: 118 us -> 105 us (0.89)
  Pallas kernels: 113 us -> 98.6 us
    pallas_call x1, Pallas kernels: 113 us -> 98.6 us  [step_call(): pl.pallas_call(functools.partial(step_kernel, n_ty, n_tx, scaling), name=...]
where the time goes in v4:
time: 105 us; the launch traced here: 103 us
  Pallas kernels  98.6 us (94%)
  local copies, waits for them, and re-layouts  4.08 us (4%)
    pallas_call x1, Pallas kernels, step_call(): pl.pallas_call(functools.partial(step_kernel, n_ty, n_tx, scaling), name=...  98.6 us
    unnamed x4, local copies, waits for them, and re-layouts  4.08 us

profile of v4, /device:TPU:1, one launch (start us, length us, event | category | flops | bytes accessed | tf_op | source)
XLA Modules:
  0.0 103.3 jit_solution(11542404070849393276)
XLA Ops:
  0.6 98.6 %step.1 = (f32[2,2,384,384]{3,2,1,0:T(8,128)}, f32[2,4,8,8,256]{4,3,2,1,0:T(8,128)}) custom-call(f32[2,2,384,384]{3,2,1,0:T(8,128)} %obj.1, f32[2,256,256]{2,1,0:T(8,128)} %probe.1, f32[256,256]{1,0:T(8,128)} %phase.1, f32[4,256,256]{2,1,0:T(8,128)} %amplitude.1, s32[2,4]{1,0:T(2,128)} %offsets.1, s32[4]{0:T(128)} %live.1, ...), custom_call_target="tpu_custom_call" | custom-call | tf_op jit(solution)/shard_map/step/pallas_call | solution.py:701
  99.2 0.0 copy-start
  99.3 3.3 %copy.12 = f32[2,2,384,384]{3,2,1,0:T(8,128)} copy(f32[2,2,384,384]{3,2,1,0:T(8,128)} %get-tuple-element.8) | data formatting | bytes 4718592
  102.5 0.0 copy-done
  102.5 0.8 copy.13
Async XLA Ops:
  99.2 3.3 %copy-start = (f32[2,4,8,8,256]{4,3,2,1,0:T(8,128)S(1)}, f32[2,4,8,8,256]{4,3,2,1,0:T(8,128)}, u32[]{:S(2)}) copy-start(f32[2,4,8,8,256]{4,3,2,1,0:T(8,128)} %get-tuple-element.5) | copy-start | bytes 1572868

commit v5 on v4

--- a/solution.py
+++ b/solution.py
@@ -120,13 +120,13 @@
     n_tx,
     scaling,
     obj,
-    probe,
-    phase,
-    amplitude,
+    probe_given,
+    phase_given,
+    amplitude_given,
     offsets,
     live,
-    tables,
-    chosen,
+    tables_given,
+    chosen_given,
     grad,
     probe_grad,
     wide_first,
@@ -147,7 +147,13 @@
     row_sums,
     outer_part,
     inner_part,
+    probe,
+    phase,
+    amplitude,
+    tables,
+    chosen,
     local_sem,
+    given_sem,
     get_send,
     get_recv,
     put_send,
@@ -247,10 +253,6 @@
             up,
         )
 
-    def start_get(s):
-        for copy in get_right(s, 0) + get_below(s) + get_right(s, 1):
-            copy.start()
-
     def relay_get(s):
         for j, copy in enumerate(get_right(s, 0)):
             copy.wait_recv()
@@ -326,40 +328,44 @@
 
         lax.fori_loop(0, patch // 64, add_rows, 0)
 
-    def out_copies(s):
-        return [
-            pltpu.make_async_copy(
-                total.at[s, :, j, pl.ds(0, tile), :],
-                grad.at[s, :, :, columns(j)],
-                out_sem.at[s, j],
-            )
-            for j in range(lane_tiles)
-        ]
+    def out_copy(s, j):
+        return pltpu.make_async_copy(
+            total.at[s, :, j, pl.ds(0, tile), :],
+            grad.at[s, :, :, columns(j)],
+            out_sem.at[s, j],
+        )
+
+    def finish_tile(s, j):
+        if j < strip_tiles:
+            put_top(s, j).wait_recv()
+
+        def add_both(block, carry):
+            rows = pl.ds(pl.multiple_of(block * 64, 64), 64)
+            for part in range(2):
+                value = total[s, part, j, rows, :] + from_above[s, part, j, rows, :]
+                if j < strip_tiles:
+                    value += from_left_tile[s, part, j, rows, :]
+                total[s, part, j, rows, :] = value
+            return carry
+
+        def add_left(block, carry):
+            rows = pl.ds(pl.multiple_of(block * 64, 64), 64)
+            for part in range(2):
+                total[s, part, j, rows, :] += from_left_tile[s, part, j, rows, :]
+            return carry
+
+        lax.fori_loop(0, patch // 64, add_both, 0)
+        if j < strip_tiles:
+            lax.fori_loop(patch // 64, tile // 64, add_left, 0)
+        out_copy(s, j).start()
 
     def finish_put(s):
         put_bottom(s).wait_recv()
         put_below(s).wait_recv()
+        for j in reversed(range(strip_tiles, lane_tiles)):
+            finish_tile(s, j)
         for j in range(strip_tiles):
-            put_top(s, j).wait_recv()
-
-        def add_rows(block, carry):
-            rows = pl.ds(pl.multiple_of(block * 64, 64), 64)
-            for part in range(2):
-                for j in range(strip_tiles):
-                    total[s, part, j, rows, :] += from_left_tile[s, part, j, rows, :]
-            return carry
-
-        def add_above(block, carry):
-            rows = pl.ds(pl.multiple_of(block * 64, 64), 64)
-            for part in range(2):
-                for j in range(lane_tiles):
-                    total[s, part, j, rows, :] += from_above[s, part, j, rows, :]
-            return carry
-
-        lax.fori_loop(0, tile // 64, add_rows, 0)
-        lax.fori_loop(0, patch // 64, add_above, 0)
-        for copy in out_copies(s):
-            copy.start()
+            finish_tile(s, j)
 
     def summed(source, destination, index, device):
         return remote(source, destination, sum_send.at[index], sum_recv.at[index], device)
@@ -490,7 +496,8 @@
         for part in (row_sum, outer_sum, inner_sum, outer_gather, row_gather):
             part[2]()
 
-    start_get(0)
+    for copy in get_right(0, 0) + get_below(0) + get_right(0, 1):
+        copy.start()
     local = [
         pltpu.make_async_copy(
             obj.at[s, :, :, columns(j)], wide[s].at[:, j, pl.ds(0, tile), :], local_sem.at[s, j]
@@ -498,7 +505,19 @@
         for s in range(layers)
         for j in range(lane_tiles)
     ]
-    for copy in local:
+    given = [
+        pltpu.make_async_copy(source, destination, given_sem.at[index])
+        for index, (source, destination) in enumerate(
+            (
+                (chosen_given, chosen),
+                (phase_given, phase),
+                (amplitude_given, amplitude),
+                (probe_given, probe),
+                (tables_given, tables),
+            )
+        )
+    ]
+    for copy in given + local:
         copy.start()
 
     def clear(q, carry):
@@ -511,6 +530,8 @@
         return carry
 
     lax.fori_loop(0, slots, clear, 0)
+    for copy in given:
+        copy.wait()
 
     def order_target(q, carry):
         target[q] = reorder(amplitude[q], chosen[0], chosen[1])
@@ -523,9 +544,12 @@
     for copy in local:
         copy.wait()
     relay_get(0)
+    for copy in get_right(1, 0):
+        copy.start()
+    finish_get(0)
+    for copy in get_below(1) + get_right(1, 1):
+        copy.start()
     sent_get(0)
-    start_get(1)
-    finish_get(0)
 
     lane = lax.broadcasted_iota(jnp.int32, (patch, LANES), 1)
 
@@ -678,12 +702,12 @@
         for j in range(strip_tiles):
             put_corner(s, j).wait_send()
             put_top(s, j).wait_send()
-        for copy in out_copies(s):
-            copy.wait()
+        for j in range(lane_tiles):
+            out_copy(s, j).wait()
 
 
 def step_call(n_ty, n_tx, scaling, *operands):
-    obj, probe, _, amplitude, _, _, _, _ = operands
+    obj, probe, phase, amplitude, _, _, tables, chosen = operands
     layers, _, tile, _ = obj.shape
     patch = probe.shape[1]
     slots = amplitude.shape[0]
@@ -705,7 +729,7 @@
             jax.ShapeDtypeStruct(obj.shape, F32),
             jax.ShapeDtypeStruct((2, n_row, n_outer, chunk, patch), F32),
         ),
-        in_specs=[whole, vmem, vmem, vmem, smem, smem, vmem, vmem],
+        in_specs=[whole, whole, whole, whole, smem, smem, whole, whole],
         out_specs=(whole, vmem),
         scratch_shapes=[
             pltpu.VMEM((2, all_tiles, tile + patch, LANES), F32),
@@ -726,7 +750,13 @@
             pltpu.VMEM((n_outer, chunk, patch), F32),
             pltpu.VMEM((n_outer, chunk, patch), F32),
             pltpu.VMEM((INNER, chunk, patch), F32),
+            pltpu.VMEM(probe.shape, F32),
+            pltpu.VMEM(phase.shape, F32),
+            pltpu.VMEM(amplitude.shape, F32),
+            pltpu.VMEM(tables.shape, BF16),
+            pltpu.VMEM(chosen.shape, BF16),
             pltpu.SemaphoreType.DMA((layers, lane_tiles)),
+            pltpu.SemaphoreType.DMA((5,)),
             pltpu.SemaphoreType.DMA((layers, gets)),
             pltpu.SemaphoreType.DMA((layers, gets)),
             pltpu.SemaphoreType.DMA((layers, puts)),

time: 105 us -> 103 us (0.981)
  Pallas kernels: 98.6 us -> 96.9 us
    pallas_call x1, Pallas kernels: 98.6 us -> 96.9 us  [step_call(): pl.pallas_call(functools.partial(step_kernel, n_ty, n_tx, scaling), name=...]
where the time goes in v5:
time: 103 us; the launch traced here: 102 us
  Pallas kernels  96.9 us (94%)
  local copies, waits for them, and re-layouts  4.08 us (4%)
    pallas_call x1, Pallas kernels, step_call(): pl.pallas_call(functools.partial(step_kernel, n_ty, n_tx, scaling), name=...  96.9 us
    unnamed x4, local copies, waits for them, and re-layouts  4.08 us

profile of v5, /device:TPU:1, one launch (start us, length us, event | category | flops | bytes accessed | tf_op | source)
XLA Modules:
  0.0 101.6 jit_solution(10344381844875966823)
XLA Ops:
  0.6 96.9 %step.1 = (f32[2,2,384,384]{3,2,1,0:T(8,128)}, f32[2,4,8,8,256]{4,3,2,1,0:T(8,128)}) custom-call(f32[2,2,384,384]{3,2,1,0:T(8,128)} %obj.1, f32[2,256,256]{2,1,0:T(8,128)} %probe_given.1, f32[256,256]{1,0:T(8,128)} %phase_given.1, f32[4,256,256]{2,1,0:T(8,128)} %amplitude_given.1, s32[2,4]{1,0:T(2,128)} %offsets.1, s32[4]{0:T(128)} %live.1, ...), custom_call_target="tpu_custom_call" | custom-call | tf_op jit(solution)/shard_map/step/pallas_call | solution.py:725
  97.5 0.0 copy-start
  97.5 3.3 %copy.12 = f32[2,2,384,384]{3,2,1,0:T(8,128)} copy(f32[2,2,384,384]{3,2,1,0:T(8,128)} %get-tuple-element.8) | data formatting | bytes 4718592
  100.8 0.0 copy-done
  100.8 0.8 copy.13
Async XLA Ops:
  97.5 3.3 %copy-start = (f32[2,4,8,8,256]{4,3,2,1,0:T(8,128)S(1)}, f32[2,4,8,8,256]{4,3,2,1,0:T(8,128)}, u32[]{:S(2)}) copy-start(f32[2,4,8,8,256]{4,3,2,1,0:T(8,128)} %get-tuple-element.5) | copy-start | bytes 1572868

commit v6 on v5

--- a/solution.py
+++ b/solution.py
@@ -158,7 +158,6 @@
     get_recv,
     put_send,
     put_recv,
-    out_sem,
     sum_send,
     sum_recv,
 ):
@@ -328,13 +327,6 @@
 
         lax.fori_loop(0, patch // 64, add_rows, 0)
 
-    def out_copy(s, j):
-        return pltpu.make_async_copy(
-            total.at[s, :, j, pl.ds(0, tile), :],
-            grad.at[s, :, :, columns(j)],
-            out_sem.at[s, j],
-        )
-
     def finish_tile(s, j):
         if j < strip_tiles:
             put_top(s, j).wait_recv()
@@ -345,19 +337,20 @@
                 value = total[s, part, j, rows, :] + from_above[s, part, j, rows, :]
                 if j < strip_tiles:
                     value += from_left_tile[s, part, j, rows, :]
-                total[s, part, j, rows, :] = value
+                grad[s, part, rows, columns(j)] = value
             return carry
 
         def add_left(block, carry):
             rows = pl.ds(pl.multiple_of(block * 64, 64), 64)
             for part in range(2):
-                total[s, part, j, rows, :] += from_left_tile[s, part, j, rows, :]
+                value = total[s, part, j, rows, :]
+                if j < strip_tiles:
+                    value += from_left_tile[s, part, j, rows, :]
+                grad[s, part, rows, columns(j)] = value
             return carry
 
         lax.fori_loop(0, patch // 64, add_both, 0)
-        if j < strip_tiles:
-            lax.fori_loop(patch // 64, tile // 64, add_left, 0)
-        out_copy(s, j).start()
+        lax.fori_loop(patch // 64, tile // 64, add_left, 0)
 
     def finish_put(s):
         put_bottom(s).wait_recv()
@@ -702,8 +695,6 @@
         for j in range(strip_tiles):
             put_corner(s, j).wait_send()
             put_top(s, j).wait_send()
-        for j in range(lane_tiles):
-            out_copy(s, j).wait()
 
 
 def step_call(n_ty, n_tx, scaling, *operands):
@@ -726,11 +717,11 @@
         functools.partial(step_kernel, n_ty, n_tx, scaling),
         name="step",
         out_shape=(
-            jax.ShapeDtypeStruct(obj.shape, F32),
-            jax.ShapeDtypeStruct((2, n_row, n_outer, chunk, patch), F32),
+            pltpu.VMEM(obj.shape, F32),
+            pltpu.VMEM((2, n_row, n_outer, chunk, patch), F32),
         ),
         in_specs=[whole, whole, whole, whole, smem, smem, whole, whole],
-        out_specs=(whole, vmem),
+        out_specs=(vmem, vmem),
         scratch_shapes=[
             pltpu.VMEM((2, all_tiles, tile + patch, LANES), F32),
             pltpu.VMEM((2, all_tiles, tile + patch, LANES), F32),
@@ -761,14 +752,42 @@
             pltpu.SemaphoreType.DMA((layers, gets)),
             pltpu.SemaphoreType.DMA((layers, puts)),
             pltpu.SemaphoreType.DMA((layers, puts)),
-            pltpu.SemaphoreType.DMA((layers, lane_tiles)),
             pltpu.SemaphoreType.DMA((sums,)),
             pltpu.SemaphoreType.DMA((sums,)),
         ],
         compiler_params=pltpu.CompilerParams(
-            collective_id=0, has_side_effects=True, vmem_limit_bytes=60 * 1024 * 1024
+            collective_id=0, has_side_effects=True, vmem_limit_bytes=57 * 1024 * 1024
         ),
     )(*operands)
+
+
+def copy_kernel(grad, shared, grad_out, shared_out, sem):
+    copies = [
+        pltpu.make_async_copy(grad.at[s, part], grad_out.at[s, part], sem.at[2 * s + part])
+        for s in range(grad.shape[0])
+        for part in range(2)
+    ]
+    copies.append(pltpu.make_async_copy(shared, shared_out, sem.at[len(copies)]))
+    for copy in copies:
+        copy.start()
+    for copy in copies:
+        copy.wait()
+
+
+def copy_call(grad, shared):
+    whole = pl.BlockSpec(memory_space=pl.ANY)
+    vmem = pl.BlockSpec(memory_space=pltpu.VMEM)
+    return pl.pallas_call(
+        copy_kernel,
+        name="hand_over",
+        out_shape=(
+            jax.ShapeDtypeStruct(grad.shape, F32),
+            jax.ShapeDtypeStruct(shared.shape, F32),
+        ),
+        in_specs=[vmem, vmem],
+        out_specs=(whole, whole),
+        scratch_shapes=[pltpu.SemaphoreType.DMA((2 * grad.shape[0] + 1,))],
+    )(grad, shared)
 
 
 def solution(mesh):
@@ -790,6 +809,9 @@
             jnp.asarray(dft_halves(patch)),
             jnp.asarray(even_odd(patch)),
         )
+        owned = pltpu.with_memory_space_constraint(owned, pltpu.VMEM)
+        shared = pltpu.with_memory_space_constraint(shared, pltpu.VMEM)
+        owned, shared = copy_call(owned, shared)
         return owned, shared.reshape(probe_wave.shape)
 
     placed = (

time: 103 us -> 99.4 us (0.965)
  local copies, waits for them, and re-layouts: 4.08 us -> 0 us
    unnamed x4 -> x0, local copies, waits for them, and re-layouts: 4.08 us -> none
    pallas_call x0 -> x1, Pallas kernels: none -> 1.62 us  [copy_call(): pl.pallas_call(copy_kernel, name='hand_over', out_shape=(jax.ShapeDtypeSt...]
    pallas_call x1, Pallas kernels: 96.9 us -> 95.8 us  [step_call(): pl.pallas_call(functools.partial(step_kernel, n_ty, n_tx, scaling), name=...]
where the time goes in v6:
time: 99.4 us; the launch traced here: 98.2 us
  Pallas kernels  97.4 us (98%)
    pallas_call x1, Pallas kernels, step_call(): pl.pallas_call(functools.partial(step_kernel, n_ty, n_tx, scaling), name=...  95.8 us

profile of v6, /device:TPU:1, one launch (start us, length us, event | category | flops | bytes accessed | tf_op | source)
XLA Modules:
  0.0 98.2 jit_solution(8392753217096561955)
XLA Ops:
  0.6 95.8 %step.1 = (f32[2,2,384,384]{3,2,1,0:T(8,128)S(1)}, f32[2,4,8,8,256]{4,3,2,1,0:T(8,128)S(1)}) custom-call(f32[2,2,384,384]{3,2,1,0:T(8,128)} %obj.1, f32[2,256,256]{2,1,0:T(8,128)} %probe_given.1, f32[256,256]{1,0:T(8,128)} %phase_given.1, f32[4,256,256]{2,1,0:T(8,128)} %amplitude_given.1, s32[2,4]{1,0:T(2,128)} %offsets.1, s32[4]{0:T(128)} %live.1, ...), custom_call_target="tpu_custom_call" | custom-call | tf_op jit(solution)/shard_map/step/pallas_call | solution.py:716
  96.4 1.6 %hand_over.1 = (f32[2,2,384,384]{3,2,1,0:T(8,128)}, f32[2,4,8,8,256]{4,3,2,1,0:T(8,128)}) custom-call(f32[2,2,384,384]{3,2,1,0:T(8,128)S(1)} %get-tuple-element.6.grad, f32[2,4,8,8,256]{4,3,2,1,0:T(8,128)S(1)} %get-tuple-element.7.shared), custom_call_target="tpu_custom_call" | custom-call | tf_op jit(solution)/shard_map/hand_over/pallas_call | solution.py:780

commit v7 on v6

--- a/solution.py
+++ b/solution.py
@@ -641,10 +641,10 @@
     strip = range(lane_tiles, all_tiles)
     own = range(lane_tiles)
 
-    gather(1, strip, 0, tile + patch)
+    gather(1, strip, tile, patch)
     start_corners(1)
+    gather(1, strip, 0, tile)
     put_bottom(1).start()
-    gather(1, own, tile, patch)
     probe_part[...] = jnp.zeros(probe_part.shape, F32)
 
     def third_layer(q, carry):
@@ -668,9 +668,11 @@
         add_corner(1, j)
     after_pair()
     put_top(1, 0).start()
-    gather(0, strip, 0, tile + patch)
+    gather(0, strip, tile, patch)
     start_corners(0)
+    gather(1, own, tile, patch)
     put_below(1).start()
+    gather(0, strip, 0, tile)
     gather(0, own, tile, patch)
     gather(1, own, 0, tile)
     after_row()

time: 99.4 us -> 99.2 us (level)
  no operation moved by 1% of the time
where the time goes in v7:
time: 99.2 us; the launch traced here: 98.2 us
  Pallas kernels  97.4 us (98%)
    pallas_call x1, Pallas kernels, step_call(): pl.pallas_call(functools.partial(step_kernel, n_ty, n_tx, scaling), name=...  95.8 us

profile of v7, /device:TPU:1, one launch (start us, length us, event | category | flops | bytes accessed | tf_op | source)
XLA Modules:
  0.0 98.2 jit_solution(3706265116318312600)
XLA Ops:
  0.6 95.8 %step.1 = (f32[2,2,384,384]{3,2,1,0:T(8,128)S(1)}, f32[2,4,8,8,256]{4,3,2,1,0:T(8,128)S(1)}) custom-call(f32[2,2,384,384]{3,2,1,0:T(8,128)} %obj.1, f32[2,256,256]{2,1,0:T(8,128)} %probe_given.1, f32[256,256]{1,0:T(8,128)} %phase_given.1, f32[4,256,256]{2,1,0:T(8,128)} %amplitude_given.1, s32[2,4]{1,0:T(2,128)} %offsets.1, s32[4]{0:T(128)} %live.1, ...), custom_call_target="tpu_custom_call" | custom-call | tf_op jit(solution)/shard_map/step/pallas_call | solution.py:718
  96.4 1.6 %hand_over.1 = (f32[2,2,384,384]{3,2,1,0:T(8,128)}, f32[2,4,8,8,256]{4,3,2,1,0:T(8,128)}) custom-call(f32[2,2,384,384]{3,2,1,0:T(8,128)S(1)} %get-tuple-element.6.grad, f32[2,4,8,8,256]{4,3,2,1,0:T(8,128)S(1)} %get-tuple-element.7.shared), custom_call_target="tpu_custom_call" | custom-call | tf_op jit(solution)/shard_map/hand_over/pallas_call | solution.py:782
